TPU v7x, 256 devices: a whole 4x4x8 slice. The times are simulated.
256 devices in a mesh: ctx: 32 (over y, x, core), head: 8 (over z).
Axes of the slice: x: 4, y: 4, z: 8, core: 2. Of those that a mesh axis runs over, the one named last changes fastest.
Arguments:
- hidden_in: bfloat16 [8192, 2048], P('ctx'), may hold values from -6 to 6
- gain_attn: float32 [2048], replicated, may hold values from 0.1 to 1.9
- w_qkv: bfloat16 [2048, 3, 2048], P(None, None, 'head'), may hold values from -0.125 to 0.125
- conv_w: float32 [4, 3, 2048], P(None, None, 'head'), may hold values from -3 to 3
- log_decay: float32 [8192, 16], P('ctx', 'head'), may hold values from -1 to 0, as said below
- norm_gain: float32 [2048], P('head'), may hold values from 0.1 to 1.9
- w_out: bfloat16 [2048, 2048], P('head'), may hold values from -0.125 to 0.125
- gain_moe: float32 [2048], replicated, may hold values from 0.1 to 1.9
- expert_ids: int32 [8192, 8], P('ctx'), may hold values from 0 to 63, all different within a row; in each aligned block of 256 rows (0 to 255, 256 to 511, ...) at most 48 rows name the same one
- route_weights: float32 [8192, 8], P('ctx'), may hold values from 0.05 to 1
- w_gate: bfloat16 [256, 2048, 256], P(('ctx', 'head')), may hold values from -0.125 to 0.125
- w_up: bfloat16 [256, 2048, 256], P(('ctx', 'head')), may hold values from -0.125 to 0.125
- w_down: bfloat16 [256, 256, 2048], P(('ctx', 'head')), may hold values from -0.1875 to 0.1875
- grad_core: bfloat16 [8192, 2048], P('ctx', 'head'), may hold values from -6 to 6
Outputs:
- layer_out: bfloat16 [8192, 2048], P('ctx', 'head')
- grad_q: bfloat16 [8192, 2048], P('ctx', 'head')
- grad_k: bfloat16 [8192, 2048], P('ctx', 'head')
- grad_v: bfloat16 [8192, 2048], P('ctx', 'head')
Inputs may be any that keep to these rules, and one draw needn't show every extreme that they name: `expert_ids`: in each aligned block of 256 rows (the tokens of one index of ctx) no expert is chosen by more than 48 rows, a bound that some block reaches; the 8 experts of a row differ. `log_decay`: every entry is negative.
All inputs are finite; a program needn't handle non-finite values.
Results may differ from a plain program's by a relative error of at most 0.023.
Values may be sent and summed in bfloat16 or wider, within the bound.
A program may use at most 128 MiB of HBM per device.

v0:
```python
import jax
import jax.numpy as jnp
from jax import lax
from jax.sharding import PartitionSpec as P

KERNEL = 4
TOP = 8
EXP_CTX = 2


def shifted(value, axis, steps):
    count = lax.axis_size(axis)
    first, last = (max(0, -steps), min(count, count - steps))
    return lax.ppermute(value, axis, [(source, source + steps) for source in range(first, last)])


def entering(value, axis, join, neutral, backward):
    count, mine = (lax.axis_size(axis), lax.axis_index(axis))
    pieces = jax.tree.map(lambda part: lax.all_gather(part, axis), value)
    if backward:
        pieces = jax.tree.map(lambda part: part[::-1], pieces)
        mine = count - 1 - mine
    total = jax.tree.map(
        lambda part, zero: jnp.full_like(part, 0) + jnp.asarray(zero, part.dtype), value, neutral
    )

    def hop(position, total):
        longer = join(total, jax.tree.map(lambda part: part[position], pieces))
        return jax.tree.map(lambda new, old: jnp.where(position < mine, new, old), longer, total)

    return lax.fori_loop(0, count - 1, hop, total)


def rms_norm(values, gain):
    return values * lax.rsqrt(jnp.mean(values * values, axis=-1, keepdims=True) + 1e-06) * gain


def link(earlier, later):
    return (earlier[0] * later[0], later[0][:, None, None] * earlier[1] + later[1])


def body(
    hidden_in,
    gain_attn,
    w_qkv,
    conv_w,
    log_decay,
    norm_gain,
    w_out,
    gain_moe,
    expert_ids,
    route_weights,
    w_gate,
    w_up,
    w_down,
    grad_core,
):
    hi = lax.Precision.HIGHEST
    n_ctx = lax.axis_size("ctx")
    n_head = lax.axis_size("head")
    my_head = lax.axis_index("head")
    tok_dev, width = hidden_in.shape
    chans = w_qkv.shape[2]
    heads_here = log_decay.shape[1]
    head_size = chans // heads_here
    experts = EXP_CTX * n_ctx
    cap = 3 * tok_dev * TOP // (2 * experts)
    shards = n_head // EXP_CTX
    local_expert = my_head // shards
    cols = width // n_head
    x_float = hidden_in.astype(jnp.float32)
    normed = rms_norm(x_float, gain_attn).astype(jnp.bfloat16)
    mixed = jnp.einsum("ti,icj->tcj", normed, w_qkv, preferred_element_type=jnp.float32).astype(
        jnp.bfloat16
    )
    rim = shifted(mixed[tok_dev - (KERNEL - 1) :], "ctx", 1)
    padded = jnp.concatenate([rim, mixed], axis=0).astype(jnp.float32)
    conv_out = jnp.zeros(mixed.shape, jnp.float32)
    for offset in range(KERNEL):
        conv_out = (
            conv_out + conv_w[offset] * padded[KERNEL - 1 - offset : KERNEL - 1 - offset + tok_dev]
        )
    activ = jax.nn.silu(conv_out)
    shape3 = (tok_dev, heads_here, head_size)
    queries = (activ[:, 0] * head_size ** (-0.5)).astype(jnp.bfloat16).reshape(shape3)
    key_rows = activ[:, 1].astype(jnp.bfloat16).reshape(shape3)
    val_rows = activ[:, 2].astype(jnp.bfloat16).reshape(shape3)
    query_f = queries.astype(jnp.float32)
    key_f = key_rows.astype(jnp.float32)
    value_f = val_rows.astype(jnp.float32)
    cot_rows = grad_core.reshape(shape3)
    cot_f = cot_rows.astype(jnp.float32)
    cum_decay = jnp.cumsum(log_decay, axis=0)
    cum_t = cum_decay.T
    diff = cum_t[:, :, None] - cum_t[:, None, :]
    lower = (jnp.arange(tok_dev)[:, None] >= jnp.arange(tok_dev)[None, :])[None]
    decay_mask = jnp.where(lower, jnp.exp(jnp.where(lower, diff, 0.0)), 0.0)
    scores = (
        jnp.einsum("thd,shd->hts", queries, key_rows, preferred_element_type=jnp.float32)
        * decay_mask
    )
    tail = jnp.exp(cum_decay[-1][None, :] - cum_decay)
    lead_decay = jnp.exp(cum_decay)
    summary = jnp.einsum("shd,she->hde", key_f * tail[:, :, None], value_f, precision=hi)
    backsum = jnp.einsum("thd,the->hde", query_f * lead_decay[:, :, None], cot_f, precision=hi)
    zeros_state = jnp.zeros((heads_here, head_size, head_size), jnp.float32)
    block_decay = jnp.exp(cum_decay[-1])
    identity = (jnp.ones((heads_here,), jnp.float32), zeros_state)
    _, state_in = entering((block_decay, summary), "ctx", link, identity, False)
    _, grad_in = entering((block_decay, backsum), "ctx", link, identity, True)
    local = jnp.einsum("hts,shd->thd", scores, value_f, precision=hi)
    carried = jnp.einsum("thd,hde->the", query_f, state_in, precision=hi) * lead_decay[:, :, None]
    attended = local + carried
    dov = (
        jnp.einsum("thd,shd->hts", cot_rows, val_rows, preferred_element_type=jnp.float32)
        * decay_mask
    )
    grad_q = jnp.einsum("hts,shd->thd", dov, key_f, precision=hi)
    grad_q = grad_q + lead_decay[:, :, None] * jnp.einsum(
        "the,hde->thd", cot_f, state_in, precision=hi
    )
    grad_k = jnp.einsum("hts,thd->shd", dov, query_f, precision=hi)
    grad_k = grad_k + tail[:, :, None] * jnp.einsum("the,hde->thd", value_f, grad_in, precision=hi)
    grad_v = jnp.einsum("hts,the->she", scores, cot_f, precision=hi)
    grad_v = grad_v + tail[:, :, None] * jnp.einsum("thd,hde->the", key_f, grad_in, precision=hi)
    headed = rms_norm(attended, norm_gain.reshape(heads_here, head_size)).reshape(tok_dev, chans)
    headed = headed.astype(jnp.bfloat16)
    partial_out = jnp.dot(headed, w_out, preferred_element_type=jnp.float32)
    attn_total = lax.psum(partial_out.astype(jnp.bfloat16), "head").astype(jnp.float32)
    resid_full = x_float + attn_total
    moe_in = rms_norm(resid_full, gain_moe).astype(jnp.bfloat16)
    resid_mine = lax.dynamic_slice_in_dim(resid_full, my_head * cols, cols, 1)
    hot = (expert_ids[:, :, None] == jnp.arange(experts, dtype=jnp.int32)).astype(jnp.int32)
    counts = jnp.sum(hot, axis=1)
    ranks = jnp.cumsum(counts, axis=0) - counts
    slot = jnp.sum(hot * ranks[:, None, :], axis=-1)
    owner = expert_ids // EXP_CTX
    local_id = expert_ids % EXP_CTX
    picked = local_id == local_expert
    source_rows = jnp.broadcast_to(moe_in[:, None, :], (tok_dev, TOP, width)).reshape(-1, width)
    total = jnp.zeros((tok_dev, width), jnp.float32)
    positions = jnp.where(picked, owner * cap + slot, n_ctx * cap).reshape(-1)
    buffer = (
        jnp.zeros((n_ctx * cap, width), jnp.bfloat16).at[positions].set(source_rows, mode="drop")
    )
    buffer = buffer.reshape(n_ctx, cap, width)
    batch = lax.all_to_all(buffer, "ctx", split_axis=0, concat_axis=0, tiled=True)
    gate_val = jnp.einsum("ncd,df->ncf", batch, w_gate[0], preferred_element_type=jnp.float32)
    up_val = jnp.einsum("ncd,df->ncf", batch, w_up[0], preferred_element_type=jnp.float32)
    inner = (jax.nn.silu(gate_val) * up_val).astype(jnp.bfloat16)
    returned = lax.all_to_all(
        jnp.einsum("ncf,fd->ncd", inner, w_down[0], preferred_element_type=jnp.float32).astype(
            jnp.bfloat16
        ),
        "ctx",
        split_axis=0,
        concat_axis=0,
        tiled=True,
    )
    flat_back = returned.reshape(n_ctx * cap, width)
    fetch = jnp.where(picked, owner * cap + slot, 0)
    weights = jnp.where(picked, route_weights, 0.0)
    for chosen in range(TOP):
        total = total + weights[:, chosen, None] * flat_back[fetch[:, chosen]].astype(jnp.float32)
    moe_out = lax.psum_scatter(
        total.astype(jnp.bfloat16), "head", scatter_dimension=1, tiled=True
    ).astype(jnp.float32)
    layer_out = (resid_mine + moe_out).astype(jnp.bfloat16)
    return (
        layer_out,
        grad_q.reshape(tok_dev, chans).astype(jnp.bfloat16),
        grad_k.reshape(tok_dev, chans).astype(jnp.bfloat16),
        grad_v.reshape(tok_dev, chans).astype(jnp.bfloat16),
    )


def solution(mesh):
    in_specs = (
        P("ctx", None),
        P(),
        P(None, None, "head"),
        P(None, None, "head"),
        P("ctx", "head"),
        P("head"),
        P("head", None),
        P(),
        P("ctx", None),
        P("ctx", None),
        P(("ctx", "head"), None, None),
        P(("ctx", "head"), None, None),
        P(("ctx", "head"), None, None),
        P("ctx", "head"),
    )
    out_specs = (P("ctx", "head"), P("ctx", "head"), P("ctx", "head"), P("ctx", "head"))
    return jax.shard_map(body, mesh=mesh, in_specs=in_specs, out_specs=out_specs, check_vma=False)
```

profile of v0, /device:TPU:32, one launch (start us, length us, event | category | flops | bytes accessed | tf_op | source)
XLA Modules:
  0.0 524.5 jit_solution(18386399533522410628)
XLA Ops:
  9.4 2.3 convolution_convert_fusion.2
  18.4 25.0 %all-gather.2 = f32[32,1,2]{2,1,0:T(1,128)S(1)} all-gather(f32[1,1,2]{2,1,0:T(1,128)S(1)} %bitcast.218), channel_id=1, replica_groups=mesh['ctx'=32,'head'=8] {'ctx'}, dimensions={0}, use_global_device_ids=true | all-gather | bytes 264 | tf_op jit(solution)/shard_map/all_gather | solution.py:19
  45.1 29.0 %all-gather.6.cloned.1.call-done = f32[64,128,128]{2,1,0:T(8,128)} async-done(((f32[2,128,128]{2,1,0:T(8,128)}), f32[64,128,128]{2,1,0:T(8,128)}) %all-gather.6.cloned.1.call-update) | async-done | bytes 4194320 | tf_op jit(solution)/shard_map/all_gather | solution.py:19
  74.0 32.2 %while.28 = (s32[]{:T(128)}, f32[2,128,128]{2,1,0:T(8,128)S(1)}, s32[]{:T(128)}, f32[32,2]{1,0:T(8,128)S(1)}, f32[32,2,128,128]{3,2,1,0:T(8,128)}, /*index=5*/s32[]{:T(128)}, s32[]{:T(128)}) while((s32[]{:T(128)}, f32[2,128,128]{2,1,0:T(8,128)S(1)}, s32[]{:T(128)}, f32[32,2]{1,0:T(8,128)S(1)}, f32[32,2,128,128]{3,2,1,0:T(8,128)}, ...), condition=%wide.region_4.5_spmd.clone, body=%wide.region_3.4_spmd.clone.sunk | while | flops 131076 | bytes 393353 | solution.py:31
  110.4 73.6 %all-reduce.2.cloned.1.call-done = bf16[256,2048]{1,0:T(8,128)(2,1)} async-done(((bf16[256,2048]{1,0:T(8,128)(2,1)}), bf16[256,2048]{1,0:T(8,128)(2,1)}) %all-reduce.2.cloned.1.call-update) | async-done | bytes 1048592 | tf_op jit(solution)/shard_map/psum | solution.py:129
  184.0 3.0 convert_add_fusion
  187.5 16.4 %scatter_custom_fusion = bf16[1536,2048]{1,0:T(8,128)(2,1)} fusion(s32[2048]{0:T(1024)} %bitcast.196, bf16[256,2048]{1,0:T(8,128)(2,1)S(1)} %multiply_convert_fusion, bf16[]{:T(256)} %constant.131.clone.1), kind=kCustom, calls=%fused_computation.15 | custom fusion | bytes 7340544 | tf_op jit(solution)/shard_map/scatter | solution.py:144
  203.9 7.4 %all-to-all-start = ((bf16[32,48,2048]{2,1,0:T(8,128)(2,1)}), bf16[32,48,2048]{2,1,0:T(8,128)(2,1)}, u32[]{:S(2)}, u32[]{:S(2)}) async-start(bf16[32,48,2048]{2,1,0:T(8,128)(2,1)} %bitcast.179), calls=%async_computation | async-start | bytes 12582912 | tf_op jit(solution)/shard_map/all_to_all | solution.py:147
  212.5 81.7 %all-to-all-done = bf16[32,48,2048]{2,1,0:T(8,128)(2,1)} async-done(((bf16[32,48,2048]{2,1,0:T(8,128)(2,1)}), bf16[32,48,2048]{2,1,0:T(8,128)(2,1)}, u32[]{:S(2)}, u32[]{:S(2)}) %all-to-all-start) | async-done | bytes 6291488 | tf_op jit(solution)/shard_map/all_to_all | solution.py:147
  294.1 5.9 %fusion.26 = f32[32,48,256]{2,1,0:T(8,128)} fusion(bf16[32,48,2048]{2,1,0:T(8,128)(2,1)} %all-to-all-done, bf16[1,2048,256]{2,1,0:T(8,128)(2,1)S(1)} %copy-done.30), kind=kOutput, calls=%fused_computation.57 | convolution fusion | flops 1610612736 | bytes 8912896 | tf_op jit(solution)/shard_map/ncd,df->ncf/dot_general | solution.py:148
  300.1 12.6 %convolution_convert_fusion = bf16[32,48,2048]{2,1,0:T(8,128)(2,1)} fusion(f32[32,48,256]{2,1,0:T(8,128)} %fusion.26, bf16[32,48,2048]{2,1,0:T(8,128)(2,1)} %all-to-all-done, bf16[1,256,2048]{2,1,0:T(8,128)(2,1)S(1)} %copy-done.31, bf16[1,2048,256]{2,1,0:T(8,128)(2,1)} %param.29), kind=kOutput, calls=%fused_computation.17 | convolution fusion | flops 3226730496 | bytes 16252928 | tf_op jit(solution)/shard_map/ncf,fd->ncd/dot_general | solution.py:152
  312.7 5.0 all-to-all-start.1
  322.9 4.6 rev.7
  327.5 68.1 %all-to-all-done.1 = bf16[32,48,2048]{2,1,0:T(8,128)(2,1)} async-done(((bf16[32,48,2048]{2,1,0:T(8,128)(2,1)}), bf16[32,48,2048]{2,1,0:T(8,128)(2,1)}, u32[]{:S(2)}, u32[]{:S(2)}) %all-to-all-start.1) | async-done | bytes 6291488 | tf_op jit(solution)/shard_map/all_to_all | solution.py:151
  395.6 6.0 %gather_fusion.7 = bf16[256,2048]{1,0:T(8,128)(2,1)S(1)} fusion(bf16[1536,2048]{1,0:T(8,128)(2,1)} %bitcast.21, s32[1024]{0:T(1024)S(1)} %pad_clamp_fusion), kind=kCustom, calls=%fused_computation.7 | custom fusion | bytes 2098176 | tf_op jit(solution)/shard_map/gather | solution.py:164
  401.6 6.0 %gather_fusion.6 = bf16[256,2048]{1,0:T(8,128)(2,1)S(1)} fusion(bf16[1536,2048]{1,0:T(8,128)(2,1)} %bitcast.21, s32[1024]{0:T(1024)S(1)} %pad_clamp_fusion.1), kind=kCustom, calls=%fused_computation.6 | custom fusion | bytes 2098176 | tf_op jit(solution)/shard_map/gather | solution.py:164
  407.6 6.0 %gather_fusion.5 = bf16[256,2048]{1,0:T(8,128)(2,1)S(1)} fusion(bf16[1536,2048]{1,0:T(8,128)(2,1)} %bitcast.21, s32[1024]{0:T(1024)S(1)} %pad_clamp_fusion.2), kind=kCustom, calls=%fused_computation.5 | custom fusion | bytes 2098176 | tf_op jit(solution)/shard_map/gather | solution.py:164
  413.5 7.1 %gather_fusion.4 = bf16[256,2048]{1,0:T(8,128)(2,1)} fusion(bf16[1536,2048]{1,0:T(8,128)(2,1)} %bitcast.21, s32[1024]{0:T(1024)} %pad_clamp_fusion.3), kind=kCustom, calls=%fused_computation.4 | custom fusion | bytes 2098176 | tf_op jit(solution)/shard_map/gather | solution.py:164
  420.6 7.3 %gather_fusion.3 = bf16[256,2048]{1,0:T(8,128)(2,1)} fusion(bf16[1536,2048]{1,0:T(8,128)(2,1)} %bitcast.21, s32[1024]{0:T(1024)} %pad_clamp_fusion.4), kind=kCustom, calls=%fused_computation.3 | custom fusion | bytes 2098176 | tf_op jit(solution)/shard_map/gather | solution.py:164
  427.9 7.1 %gather_fusion.2 = bf16[256,2048]{1,0:T(8,128)(2,1)} fusion(bf16[1536,2048]{1,0:T(8,128)(2,1)} %bitcast.21, s32[1024]{0:T(1024)} %pad_clamp_fusion.5), kind=kCustom, calls=%fused_computation.2 | custom fusion | bytes 2098176 | tf_op jit(solution)/shard_map/gather | solution.py:164
  435.0 7.1 %gather_fusion.1 = bf16[256,2048]{1,0:T(8,128)(2,1)} fusion(bf16[1536,2048]{1,0:T(8,128)(2,1)} %bitcast.21, s32[1024]{0:T(1024)} %pad_clamp_fusion.6), kind=kCustom, calls=%fused_computation.1 | custom fusion | bytes 2098176 | tf_op jit(solution)/shard_map/gather | solution.py:164
  442.0 7.0 %gather_fusion = bf16[256,2048]{1,0:T(8,128)(2,1)} fusion(bf16[1536,2048]{1,0:T(8,128)(2,1)} %bitcast.21, s32[1024]{0:T(1024)S(1)} %pad_clamp_fusion.7), kind=kCustom, calls=%fused_computation | custom fusion | bytes 2098176 | tf_op jit(solution)/shard_map/gather | solution.py:164
  449.0 4.6 add_convert_fusion
  453.7 52.9 %while.29 = (s32[]{:T(128)}, f32[2,128,128]{2,1,0:T(8,128)S(1)}, s32[]{:T(128)}, f32[32,2]{1,0:T(8,128)}, f32[32,2,128,128]{3,2,1,0:T(8,128)}, /*index=5*/s32[]{:T(128)}, s32[]{:T(128)}) while((s32[]{:T(128)}, f32[2,128,128]{2,1,0:T(8,128)S(1)}, s32[]{:T(128)}, f32[32,2]{1,0:T(8,128)}, f32[32,2,128,128]{3,2,1,0:T(8,128)}, ...), condition=%wide.region_15.16_spmd.clone, body=%wide.region_14.15_spmd.clone.sunk | while | flops 131076 | bytes 393353 | solution.py:31
  (275 shorter events, 115.3 us)
Async XLA Ops:
  7.2 66.8 %all-gather.6.cloned.1.call-start = ((), (), s32[]{:S(2)}) async-start(), calls=%async_computation.5 | async-start | bytes 4325376 | tf_op jit(solution)/shard_map/all_gather | solution.py:19
  12.4 3.1 collective-permute-start
  15.2 29.5 %copy-start.25 = (f32[1,2,2,128]{3,1,2,0:T(2,128)}, f32[1,2,2,128]{3,1,2,0:T(2,128)S(1)}, u32[]{:S(2)}) copy-start(f32[1,2,2,128]{3,1,2,0:T(2,128)S(1)} %copy.239) | copy-start | bytes 6148
  17.2 56.8 %copy-start.9 = (bf16[256,2,128]{2,1,0:T(2,128)(2,1)}, bf16[256,2,128]{2,1,0:T(2,128)(2,1)S(1)}, u32[]{:S(2)}) copy-start(bf16[256,2,128]{2,1,0:T(2,128)(2,1)S(1)} %convert_element_type.119) | copy-start | bytes 393220
  17.4 27.2 %copy-start.11 = (bf16[256,2,128]{0,2,1:T(8,128)(2,1)}, bf16[256,2,128]{0,2,1:T(8,128)(2,1)S(1)}, u32[]{:S(2)}) copy-start(bf16[256,2,128]{0,2,1:T(8,128)(2,1)S(1)} %copy.176) | copy-start | bytes 393220
  18.3 165.6 %all-reduce.2.cloned.1.call-start = ((), (), s32[]{:S(2)}) async-start(), calls=%async_computation.3 | async-start | bytes 2097152 | tf_op jit(solution)/shard_map/psum | solution.py:129
  43.5 30.5 %copy-start.20 = (f32[32,1,2]{0,2,1:T(2,128)}, f32[32,1,2]{0,2,1:T(2,128)S(1)}, u32[]{:S(2)}) copy-start(f32[32,1,2]{0,2,1:T(2,128)S(1)} %copy.175) | copy-start | bytes 772
  44.5 62.1 %copy-start.24 = (s32[64,3]{0,1:T(4,128)}, s32[64,3]{0,1:T(4,128)S(1)}, u32[]{:S(2)}) copy-start(s32[64,3]{0,1:T(4,128)S(1)} %reduce-window.19) | copy-start | bytes 2308
  44.6 62.0 %copy-start.16 = (pred[256,256]{1,0:T(8,128)(4,1)}, pred[256,256]{1,0:T(8,128)(4,1)S(1)}, u32[]{:S(2)}) copy-start(pred[256,256]{1,0:T(8,128)(4,1)S(1)} %iota_compare_fusion.1) | copy-start | bytes 196612
  44.7 166.8 %copy-start.6 = (bf16[256,1,256]{0,2,1:T(8,128)(2,1)}, bf16[256,1,256]{0,2,1:T(8,128)(2,1)S(1)}, u32[]{:S(2)}) copy-start(bf16[256,1,256]{0,2,1:T(8,128)(2,1)S(1)} %copy.207) | copy-start | bytes 393220
  45.0 62.1 %copy-start.4 = (f32[2,256,256]{2,1,0:T(8,128)}, f32[2,256,256]{2,1,0:T(8,128)S(1)}, u32[]{:S(2)}) copy-start(f32[2,256,256]{2,1,0:T(8,128)S(1)} %convolution_multiply_fusion) | copy-start | bytes 1572868
  45.0 62.1 %copy-start.29 = (f32[256]{0:T(256)S(1)}, f32[256]{0:T(256)}, u32[]{:S(2)}) copy-start(f32[256]{0:T(256)} %param.23) | copy-start | bytes 3076
  74.0 33.2 %copy-start.12 = (bf16[256,2048]{1,0:T(8,128)(2,1)S(1)}, bf16[256,2048]{1,0:T(8,128)(2,1)}, u32[]{:S(2)}) copy-start(bf16[256,2048]{1,0:T(8,128)(2,1)} %param.24) | copy-start | bytes 3145732
  107.1 76.9 %copy-start.2 = (bf16[256,2048]{1,0:T(8,128)(2,1)S(1)}, bf16[256,2048]{1,0:T(8,128)(2,1)}, u32[]{:S(2)}) copy-start(bf16[256,2048]{1,0:T(8,128)(2,1)} %param.18) | copy-start | bytes 3145732
  203.9 90.2 %copy-start.30 = (bf16[1,2048,256]{2,1,0:T(8,128)(2,1)S(1)}, bf16[1,2048,256]{2,1,0:T(8,128)(2,1)}, u32[]{:S(2)}) copy-start(bf16[1,2048,256]{2,1,0:T(8,128)(2,1)} %param.28) | copy-start | bytes 3145732
  203.9 90.2 %all-to-all-start = ((bf16[32,48,2048]{2,1,0:T(8,128)(2,1)}), bf16[32,48,2048]{2,1,0:T(8,128)(2,1)}, u32[]{:S(2)}, u32[]{:S(2)}) async-start(bf16[32,48,2048]{2,1,0:T(8,128)(2,1)} %bitcast.179), calls=%async_computation | async-start | bytes 12582912 | tf_op jit(solution)/shard_map/all_to_all | solution.py:147
  211.3 111.6 %all-gather.8.cloned.1.call-start = ((), (), s32[]{:S(2)}) async-start(), calls=%async_computation.6 | async-start | bytes 4325376 | tf_op jit(solution)/shard_map/all_gather | solution.py:19
  211.5 110.4 %copy-start.7 = (bf16[256,256]{0,1:T(8,128)(2,1)}, bf16[256,256]{0,1:T(8,128)(2,1)S(1)}, u32[]{:S(2)}) copy-start(bf16[256,256]{0,1:T(8,128)(2,1)S(1)} %copy.208) | copy-start | bytes 393220
  212.4 87.6 %copy-start.31 = (bf16[1,256,2048]{2,1,0:T(8,128)(2,1)S(1)}, bf16[1,256,2048]{2,1,0:T(8,128)(2,1)}, u32[]{:S(2)}) copy-start(bf16[1,256,2048]{2,1,0:T(8,128)(2,1)} %param.30) | copy-start | bytes 3145732
  312.7 83.0 %all-to-all-start.1 = ((bf16[32,48,2048]{2,1,0:T(8,128)(2,1)}), bf16[32,48,2048]{2,1,0:T(8,128)(2,1)}, u32[]{:S(2)}, u32[]{:S(2)}) async-start(bf16[32,48,2048]{2,1,0:T(8,128)(2,1)} %convolution_convert_fusion), calls=%async_computation.1 | async-start | bytes 12582912 | tf_op jit(solution)/shard_map/all_to_all | solution.py:151
  317.7 198.0 %reduce-scatter.2.cloned.1.call-start = ((), (), s32[]{:S(2)}) async-start(), calls=%async_computation.4 | async-start | bytes 1179648 | tf_op jit(solution)/shard_map/reduce_scatter | solution.py:165
  453.6 53.0 %copy-start.10 = (bf16[256,2,128]{2,1,0:T(2,128)(2,1)S(1)}, bf16[256,2,128]{2,1,0:T(2,128)(2,1)}, u32[]{:S(2)}) copy-start(bf16[256,2,128]{2,1,0:T(2,128)(2,1)} %copy-done.9) | copy-start | bytes 393220
  453.6 53.3 %copy-start.5 = (f32[2,256,256]{2,1,0:T(8,128)S(1)}, f32[2,256,256]{2,1,0:T(8,128)}, u32[]{:S(2)}) copy-start(f32[2,256,256]{2,1,0:T(8,128)} %copy-done.4) | copy-start | bytes 1572868
  453.6 53.3 %copy-start.8 = (bf16[256,256]{0,1:T(8,128)(2,1)S(1)}, bf16[256,256]{0,1:T(8,128)(2,1)}, u32[]{:S(2)}) copy-start(bf16[256,256]{0,1:T(8,128)(2,1)} %copy-done.7) | copy-start | bytes 393220
  (16 other events, 106.3 us)
Sparse Core Ops, SparseCore 0:
  18.5 55.5 all-gather.5
  108.9 75.0 all-reduce.1
  215.3 86.4 all-gather.7
  453.8 31.1 reduce-scatter.1
where the time goes:
time: 535 us; the launch traced here: 524 us
  waiting for transfers between devices  252 us (47%)
  local copies, waits for them, and re-layouts  104 us (19%)
  other arithmetic  80.3 us (15%)
  matrix products  32 us (6%)
  blocking collectives  25 us (5%)
  between operations  14.9 us (3%)
  starting transfers between devices  14.4 us (3%)
    all_to_all x1, waiting for transfers between devices, body(): lax.all_to_all(buffer, 'ctx', split_axis=0, concat_axis=0, tiled=True)  81.7 us
    psum x1, waiting for transfers between devices, body(): lax.psum(partial_out.astype(jnp.bfloat16), 'head').astype(jnp.float32)  73.6 us
    all_to_all x1, waiting for transfers between devices, body(): lax.all_to_all(jnp.einsum('ncf,fd->ncd', inner, w_down[0], preferred_elem...  68.1 us
    select_n x62, other arithmetic, hop(): jnp.where(position < mine, new, old)  61.6 us
    gather x8, local copies, waits for them, and re-layouts, body(): flat_back[fetch[:, chosen]].astype(jnp.float32)  53.3 us
    all_gather x2, waiting for transfers between devices, entering(): pieces = jax.tree.map(lambda part: lax.all_gather(part, axis), value)  29 us
    all_gather x1, blocking collectives, entering(): pieces = jax.tree.map(lambda part: lax.all_gather(part, axis), value)  25 us
    mul x62, local copies, waits for them, and re-layouts, link(): later[0][:, None, None] * earlier[1] + later[1]  21.8 us
  transfers between devices with their start and end apart: 7, of which 4 were waited for; matrix products, arithmetic and copies ran while one was open for 18% of the time, Pallas kernels for 0%

commit v1 on v0

v1 whole, which is shorter than its diff:
```python
import functools

import jax
import jax.numpy as jnp
from jax import lax
from jax.experimental import pallas as pl
from jax.experimental.pallas import tpu as pltpu
from jax.sharding import PartitionSpec as P

KERNEL = 4
TOP = 8
EXP_CTX = 2
MESH = pl.DeviceIdType.MESH
BF = jnp.bfloat16
F32 = jnp.float32


def shifted(value, axis, steps):
    count = lax.axis_size(axis)
    first, last = (max(0, -steps), min(count, count - steps))
    return lax.ppermute(value, axis, [(source, source + steps) for source in range(first, last)])


def rms_norm(values, gain):
    return values * lax.rsqrt(jnp.mean(values * values, axis=-1, keepdims=True) + 1e-06) * gain


def greet(axis, n, me, offsets):
    barrier = pltpu.get_barrier_semaphore()
    for r in offsets:
        pl.semaphore_signal(
            barrier, inc=1, device_id={axis: lax.rem(me + r, n)}, device_id_type=MESH
        )
    pl.semaphore_wait(barrier, len(offsets))


def state_kernel(n, rows, give, fwd_out, bwd_out, got, back, land, s1, r1, s2, r2):
    me = lax.axis_index("ctx")
    greet("ctx", n, me, range(1, n))

    def push(source, target, send_sem, recv_sem, r):
        peer = lax.rem(me + r, n)
        return pltpu.make_async_remote_copy(
            src_ref=source.at[peer],
            dst_ref=target.at[me],
            send_sem=send_sem.at[r - 1],
            recv_sem=recv_sem.at[r - 1],
            device_id={"ctx": peer},
            device_id_type=MESH,
        )

    first = [push(give, got, s1, r1, r) for r in range(1, n)]
    for copy in first:
        copy.start()
    got[me] = give[me]
    for copy in first:
        copy.wait()
    state = jnp.zeros((rows, give.shape[2]), F32)
    for k in range(n):
        back[k, 0:rows] = state
        state = got[k, 0:rows] + got[k, 2 * rows : 3 * rows] * state
    state = jnp.zeros((rows, give.shape[2]), F32)
    for k in range(n - 1, -1, -1):
        back[k, rows : 2 * rows] = state
        state = got[k, rows : 2 * rows] + got[k, 2 * rows : 3 * rows] * state
    second = [push(back, land, s2, r2, r) for r in range(1, n)]
    for copy in second:
        copy.start()
    land[me] = back[me]
    for copy in second:
        copy.wait()
    fwd_out[...] = land[:, 0:rows]
    bwd_out[...] = land[:, rows : 2 * rows]


def state_exchange(summary, backsum, block_decay, n):
    heads, size, _ = summary.shape
    rows = heads * size // n
    decay = jnp.broadcast_to(block_decay[:, None, None], (heads, n // heads * rows, size))
    give = jnp.concatenate(
        [
            summary.reshape(n, rows, size),
            backsum.reshape(n, rows, size),
            decay.reshape(n, rows, size),
        ],
        axis=1,
    )
    out = jax.ShapeDtypeStruct((n, rows, size), F32)
    vmem = pl.BlockSpec(memory_space=pltpu.VMEM)
    fwd, bwd = pl.pallas_call(
        functools.partial(state_kernel, n, rows),
        out_shape=(out, out),
        in_specs=[vmem],
        out_specs=(vmem, vmem),
        scratch_shapes=[
            pltpu.VMEM((n, 3 * rows, size), F32),
            pltpu.VMEM((n, 2 * rows, size), F32),
            pltpu.VMEM((n, 2 * rows, size), F32),
        ]
        + [pltpu.SemaphoreType.DMA((n - 1,))] * 4,
        compiler_params=pltpu.CompilerParams(collective_id=1, has_side_effects=True),
        name="state_exchange",
    )(give)
    return fwd.reshape(heads, size, size), bwd.reshape(heads, size, size)


def ring_kernel(n, subs, part, out, right_in, left_in, rs_s, rs_r, ag_s, ag_r):
    me = lax.axis_index("head")
    right, left = lax.rem(me + 1, n), lax.rem(me + n - 1, n)
    greet("head", n, me, (1, n - 1))
    tokens = part.shape[1]
    piece = tokens // (2 * subs)
    ways = ((right, 1, right_in), (left, -1, left_in))

    def span(way, sub):
        return pl.ds((way * subs + sub) * piece, piece)

    def reduce_copy(way, sub, step):
        peer, sign, land = ways[way]
        if step == 0:
            source = part.at[lax.rem(me - sign + n, n), span(way, sub)]
        else:
            source = land.at[step - 1, sub]
        return pltpu.make_async_remote_copy(
            src_ref=source,
            dst_ref=land.at[step, sub],
            send_sem=rs_s.at[way, step, sub],
            recv_sem=rs_r.at[way, step, sub],
            device_id={"head": peer},
            device_id_type=MESH,
        )

    sends = {}
    for sub in range(subs):
        for way in range(2):
            sends[way, sub, 0] = reduce_copy(way, sub, 0)
            sends[way, sub, 0].start()

    def gather_copy(half, sub, way, step):
        peer, sign, _ = ways[way]
        block = lax.rem(me - sign * step + 2 * n, n)
        view = out.at[block, span(half, sub)]
        return pltpu.make_async_remote_copy(
            src_ref=view,
            dst_ref=view,
            send_sem=ag_s.at[half, sub, way, step],
            recv_sem=ag_r.at[half, sub, way, step],
            device_id={"head": peer},
            device_id_type=MESH,
        )

    def hops(half, way):
        return n // 2 if half == way else n // 2 - 1

    gathers = []
    for step in range(n - 1):
        for sub in range(subs):
            for way in range(2):
                _, sign, land = ways[way]
                sends[way, sub, step].wait_recv()
                block = lax.rem(me - sign * (step + 2) + 2 * n, n)
                total = land[step, sub].astype(F32) + part[block, span(way, sub)].astype(F32)
                if step < n - 2:
                    land[step, sub] = total.astype(BF)
                    sends[way, sub, step + 1] = reduce_copy(way, sub, step + 1)
                    sends[way, sub, step + 1].start()
                else:
                    out[me, span(way, sub)] = total.astype(BF)
                    for onward in range(2):
                        copy = gather_copy(way, sub, onward, 0)
                        copy.start()
                        gathers.append(copy)
    for step in range(n // 2):
        for sub in range(subs):
            for half in range(2):
                for way in range(2):
                    if step < hops(half, way):
                        gather_copy(half, sub, way, step).wait_recv()
                        if step + 1 < hops(half, way):
                            copy = gather_copy(half, sub, way, step + 1)
                            copy.start()
                            gathers.append(copy)
    for copy in gathers:
        copy.wait_send()
    for copy in sends.values():
        copy.wait_send()


def ring_sum(part, subs=2):
    n, tokens, cols = part.shape
    piece = tokens // (2 * subs)
    vmem = pl.BlockSpec(memory_space=pltpu.VMEM)
    return pl.pallas_call(
        functools.partial(ring_kernel, n, subs),
        out_shape=jax.ShapeDtypeStruct(part.shape, BF),
        in_specs=[vmem],
        out_specs=vmem,
        scratch_shapes=[
            pltpu.VMEM((n - 1, subs, piece, cols), BF),
            pltpu.VMEM((n - 1, subs, piece, cols), BF),
            pltpu.SemaphoreType.DMA((2, n - 1, subs)),
            pltpu.SemaphoreType.DMA((2, n - 1, subs)),
            pltpu.SemaphoreType.DMA((2, subs, 2, n // 2)),
            pltpu.SemaphoreType.DMA((2, subs, 2, n // 2)),
        ],
        compiler_params=pltpu.CompilerParams(collective_id=2, has_side_effects=True),
        name="ring_sum",
    )(part)


def mm(spec, a, b):
    return jnp.einsum(spec, a.astype(BF), b.astype(BF), preferred_element_type=F32)


def body(
    hidden_in,
    gain_attn,
    w_qkv,
    conv_w,
    log_decay,
    norm_gain,
    w_out,
    gain_moe,
    expert_ids,
    route_weights,
    w_gate,
    w_up,
    w_down,
    grad_core,
):
    n_ctx = lax.axis_size("ctx")
    n_head = lax.axis_size("head")
    my_head = lax.axis_index("head")
    tok_dev, width = hidden_in.shape
    chans = w_qkv.shape[2]
    heads_here = log_decay.shape[1]
    head_size = chans // heads_here
    experts = EXP_CTX * n_ctx
    cap = 3 * tok_dev * TOP // (2 * experts)
    shards = n_head // EXP_CTX
    local_expert = my_head // shards
    cols = width // n_head
    x_float = hidden_in.astype(F32)
    normed = rms_norm(x_float, gain_attn).astype(BF)
    mixed = jnp.einsum("ti,icj->tcj", normed, w_qkv, preferred_element_type=F32).astype(BF)
    rim = shifted(mixed[tok_dev - (KERNEL - 1) :], "ctx", 1)
    padded = jnp.concatenate([rim, mixed], axis=0).astype(F32)
    conv_out = jnp.zeros(mixed.shape, F32)
    for offset in range(KERNEL):
        conv_out = (
            conv_out + conv_w[offset] * padded[KERNEL - 1 - offset : KERNEL - 1 - offset + tok_dev]
        )
    activ = jax.nn.silu(conv_out)
    shape3 = (tok_dev, heads_here, head_size)
    queries = (activ[:, 0] * head_size ** (-0.5)).astype(BF).reshape(shape3)
    keys = activ[:, 1].astype(BF).reshape(shape3)
    vals = activ[:, 2].astype(BF).reshape(shape3)
    cots = grad_core.reshape(shape3)
    steps = jnp.arange(tok_dev)
    cum_decay = jnp.cumsum(log_decay, axis=0)
    cum_t = cum_decay.T
    diff = cum_t[:, :, None] - cum_t[:, None, :]
    lower = (steps[:, None] >= steps[None, :])[None]
    decay_mask = jnp.where(lower, jnp.exp(jnp.where(lower, diff, 0.0)), 0.0)
    tail = jnp.exp(cum_decay[-1][None, :] - cum_decay)[:, :, None]
    lead = jnp.exp(cum_decay)[:, :, None]
    summary = mm("shd,she->hde", keys * tail, vals)
    backsum = mm("thd,the->hde", queries * lead, cots)
    block_decay = jnp.exp(cum_decay[-1])
    state_in, grad_in = state_exchange(summary, backsum, block_decay, n_ctx)
    scores = (mm("thd,shd->hts", queries, keys) * decay_mask).astype(BF)
    attended = mm("hts,shd->thd", scores, vals) + mm("thd,hde->the", queries, state_in) * lead
    headed = rms_norm(attended, norm_gain.reshape(heads_here, head_size)).reshape(tok_dev, chans)
    partial_out = mm("ti,izc->ztc", headed, w_out.reshape(chans, n_head, cols)).astype(BF)
    attn_total = ring_sum(partial_out)

    dov = (mm("thd,shd->hts", cots, vals) * decay_mask).astype(BF)
    grad_q = mm("hts,shd->thd", dov, keys) + lead * mm("the,hde->thd", cots, state_in)
    grad_k = mm("hts,thd->shd", dov, queries) + tail * mm("the,hde->thd", vals, grad_in)
    grad_v = mm("hts,the->she", scores, cots) + tail * mm("thd,hde->the", keys, grad_in)

    resid_full = x_float + attn_total.transpose(1, 0, 2).reshape(tok_dev, width).astype(F32)
    moe_in = rms_norm(resid_full, gain_moe).astype(BF)
    resid_mine = lax.dynamic_slice_in_dim(resid_full, my_head * cols, cols, 1)

    wanted = EXP_CTX * jnp.arange(n_ctx, dtype=jnp.int32)[:, None] + local_expert
    chosen = expert_ids.T[:, None, :] == wanted[None]
    hot = jnp.any(chosen, axis=0)
    earlier = (steps[:, None] < steps[None, :]).astype(BF)
    ranks = mm("et,tu->eu", hot.astype(BF), earlier).astype(jnp.int32)
    slot = jnp.where(hot, ranks, -1)
    weight = jnp.sum(jnp.where(chosen, route_weights.T[:, None, :], 0.0), axis=0)
    taken = slot[:, None, :] == jnp.arange(cap, dtype=jnp.int32)[None, :, None]
    pick = taken.astype(BF)
    share = jnp.where(taken, weight[:, None, :], 0.0).astype(BF)

    buffer = mm("ost,td->osd", pick, moe_in).astype(BF)
    batch = lax.all_to_all(buffer, "ctx", split_axis=0, concat_axis=0, tiled=True)
    gate_val = jnp.einsum("ncd,df->ncf", batch, w_gate[0], preferred_element_type=F32)
    up_val = jnp.einsum("ncd,df->ncf", batch, w_up[0], preferred_element_type=F32)
    inner = (jax.nn.silu(gate_val) * up_val).astype(BF)
    returned = lax.all_to_all(
        jnp.einsum("ncf,fd->ncd", inner, w_down[0], preferred_element_type=F32).astype(BF),
        "ctx",
        split_axis=0,
        concat_axis=0,
        tiled=True,
    )
    total = mm("ost,osd->td", share, returned)
    moe_out = lax.psum_scatter(total.astype(BF), "head", scatter_dimension=1, tiled=True).astype(
        F32
    )
    layer_out = (resid_mine + moe_out).astype(BF)
    return (
        layer_out,
        grad_q.reshape(tok_dev, chans).astype(BF),
        grad_k.reshape(tok_dev, chans).astype(BF),
        grad_v.reshape(tok_dev, chans).astype(BF),
    )


def solution(mesh):
    in_specs = (
        P("ctx", None),
        P(),
        P(None, None, "head"),
        P(None, None, "head"),
        P("ctx", "head"),
        P("head"),
        P("head", None),
        P(),
        P("ctx", None),
        P("ctx", None),
        P(("ctx", "head"), None, None),
        P(("ctx", "head"), None, None),
        P(("ctx", "head"), None, None),
        P("ctx", "head"),
    )
    out_specs = (P("ctx", "head"), P("ctx", "head"), P("ctx", "head"), P("ctx", "head"))
    return jax.shard_map(body, mesh=mesh, in_specs=in_specs, out_specs=out_specs, check_vma=False)
```

time: 535 us -> 343 us (0.64)
  the two profiles are of different devices: /device:TPU:32 before, /device:TPU:10 now
where the time goes in v1:
time: 343 us; the launch traced here: 342 us
  waiting for transfers between devices  95.9 us (28%)
  blocking collectives  76.7 us (22%)
  Pallas kernels  67.3 us (20%)
  matrix products  39.3 us (11%)
  local copies, waits for them, and re-layouts  19.4 us (6%)
  other arithmetic  19 us (6%)
  between operations  14.4 us (4%)
  starting transfers between devices  10.1 us (3%)
    all_to_all x1, blocking collectives, body(): lax.all_to_all(buffer, 'ctx', split_axis=0, concat_axis=0, tiled=True)  76.7 us
    all_to_all x1, waiting for transfers between devices, body(): lax.all_to_all(jnp.einsum('ncf,fd->ncd', inner, w_down[0], preferred_elem...  74.2 us
    pallas_call x1, Pallas kernels, ring_sum(): pl.pallas_call(functools.partial(ring_kernel, n, subs), out_shape=jax.Sha...  46.1 us
    reduce_scatter x1, waiting for transfers between devices, body(): lax.psum_scatter(total.astype(BF), 'head', scatter_dimension=1, tiled=True)  21.7 us
    pallas_call x1, Pallas kernels, state_exchange(): pl.pallas_call(functools.partial(state_kernel, n, rows), out_shape=(out,...  21.2 us
    dot_general x16, matrix products, mm(): jnp.einsum(spec, a.astype(BF), b.astype(BF), preferred_element_type=F32)  21.1 us
    dot_general x1, matrix products, body(): jnp.einsum('ncf,fd->ncd', inner, w_down[0], preferred_element_type=F32)  12.8 us
    unnamed x46, local copies, waits for them, and re-layouts  8.31 us
  transfers between devices with their start and end apart: 3, of which 2 were waited for; matrix products, arithmetic and copies ran while one was open for 5% of the time, Pallas kernels for 0%

profile of v1, /device:TPU:10, one launch (start us, length us, event | category | flops | bytes accessed | tf_op | source)
XLA Modules:
  0.0 342.1 jit_solution(13031656071051945109)
XLA Ops:
  7.2 1.7 fusion.1
  9.4 2.3 convolution_convert_fusion.3
  12.5 1.9 collective-permute-start
  23.0 1.6 fusion.44
  28.4 21.2 %state_exchange.1 = (f32[32,8,128]{2,1,0:T(8,128)}, f32[32,8,128]{2,1,0:T(8,128)}) custom-call(f32[32,24,128]{2,1,0:T(8,128)} %pad_maximum_fusion.give), custom_call_target="tpu_custom_call" | custom-call | tf_op jit(solution)/shard_map/state_exchange/pallas_call | solution.py:90
  53.6 1.4 fusion.4.part
  55.1 46.1 %ring_sum.1 = bf16[8,256,256]{2,1,0:T(8,128)(2,1)} custom-call(bf16[8,256,256]{2,1,0:T(8,128)(2,1)} %fusion.4.part), custom_call_target="tpu_custom_call" | custom-call | tf_op jit(solution)/shard_map/ring_sum/pallas_call | solution.py:193
  101.1 2.8 convert_bitcast_fusion
  103.9 2.9 copy.140
  106.8 2.9 copy.141
  109.7 2.2 multiply_reduce_fusion
  112.0 1.9 convolution_convert_fusion.1
  113.9 76.7 %all_to_all.10 = bf16[32,48,2048]{2,1,0:T(8,128)(2,1)S(1)} all-to-all(bf16[32,48,2048]{2,1,0:T(8,128)(2,1)S(1)} %convolution_convert_fusion.1), channel_id=1, replica_groups=mesh['ctx'=32,'head'=8] {'ctx'}, dimensions={0} | all-to-all | bytes 12582912 | tf_op jit(solution)/shard_map/all_to_all | solution.py:298
  190.6 2.6 copy-done.2
  193.3 3.0 fusion.29
  196.3 12.8 %convolution_convert_fusion = bf16[32,48,2048]{2,1,0:T(8,128)(2,1)} fusion(f32[32,48,256]{2,1,0:T(8,128)} %fusion.29, bf16[32,48,2048]{2,1,0:T(8,128)(2,1)} %copy-done.2, bf16[1,256,2048]{2,1,0:T(8,128)(2,1)} %param.26, bf16[1,2048,256]{2,1,0:T(8,128)(2,1)} %param.25), kind=kOutput, calls=%fused_computation | convolution fusion | flops 3226730496 | bytes 16252928 | tf_op jit(solution)/shard_map/ncf,fd->ncd/dot_general | solution.py:303
  209.2 8.1 %all-to-all-start.1 = ((bf16[32,48,2048]{2,1,0:T(8,128)(2,1)}), bf16[32,48,2048]{2,1,0:T(8,128)(2,1)}, u32[]{:S(2)}, u32[]{:S(2)}) async-start(bf16[32,48,2048]{2,1,0:T(8,128)(2,1)} %convolution_convert_fusion), calls=%async_computation.1 | async-start | bytes 12582912 | tf_op jit(solution)/shard_map/all_to_all | solution.py:302
  217.3 1.4 fusion.43
  218.8 74.2 %all-to-all-done.1 = bf16[32,48,2048]{2,1,0:T(8,128)(2,1)} async-done(((bf16[32,48,2048]{2,1,0:T(8,128)(2,1)}), bf16[32,48,2048]{2,1,0:T(8,128)(2,1)}, u32[]{:S(2)}, u32[]{:S(2)}) %all-to-all-start.1) | async-done | bytes 6291488 | tf_op jit(solution)/shard_map/all_to_all | solution.py:302
  292.9 5.6 %fusion = bf16[256,2048]{1,0:T(8,128)(2,1)} fusion(bf16[32,48,2048]{2,1,0:T(8,128)(2,1)} %all-to-all-done.1, bf16[32,256]{1,0:T(8,128)(2,1)} %fusion.43, s32[32,256]{1,0:T(8,128)} %fusion.19), kind=kOutput, calls=%fused_computation.6 | convolution fusion | flops 1611923456 | bytes 7389184 | tf_op jit(solution)/shard_map/ost,osd->td/dot_general | solution.py:212
  300.7 1.8 fusion.18
  302.5 1.7 copy.154
  311.9 21.7 %reduce-scatter.2.cloned.1.call-done = bf16[256,256]{1,0:T(8,128)(2,1)} async-done(((bf16[256,2048]{1,0:T(8,128)(2,1)}), bf16[256,256]{1,0:T(8,128)(2,1)}) %reduce-scatter.2.cloned.1.call-update) | async-done | bytes 131088 | tf_op jit(solution)/shard_map/reduce_scatter | solution.py:310
  333.6 1.7 add_convert_fusion
  (90 shorter events, 27.3 us)
Async XLA Ops:
  7.2 2.2 copy-start
  9.4 5.0 %copy-start.16 = (f32[256,2]{0,1:T(2,128)S(1)}, f32[256,2]{0,1:T(2,128)}, u32[]{:S(2)}) copy-start(f32[256,2]{0,1:T(2,128)} %param.18) | copy-start | bytes 6148
  9.4 6.4 %copy-start.13 = (f32[4,3,256]{2,0,1:T(4,128)S(1)}, f32[4,3,256]{2,0,1:T(4,128)}, u32[]{:S(2)}) copy-start(f32[4,3,256]{2,0,1:T(4,128)} %param.17) | copy-start | bytes 36868
  9.4 6.4 %copy-start.12 = (s32[256,8]{0,1:T(8,128)S(1)}, s32[256,8]{0,1:T(8,128)}, u32[]{:S(2)}) copy-start(s32[256,8]{0,1:T(8,128)} %param.22) | copy-start | bytes 24580
  9.4 8.6 %copy-start.10 = (bf16[256,256]{1,0:T(8,128)(2,1)S(1)}, bf16[256,256]{1,0:T(8,128)(2,1)}, u32[]{:S(2)}) copy-start(bf16[256,256]{1,0:T(8,128)(2,1)} %param.27) | copy-start | bytes 393220
  11.7 0.7 copy-start.9
  12.5 5.6 %collective-permute-start = (bf16[3,3,256]{2,0,1:T(4,128)(2,1)S(1)}, bf16[3,3,256]{2,0,1:T(4,128)(2,1)S(1)}, u32[]{:S(2)}, u32[]{:S(2)}) collective-permute-start(bf16[3,3,256]{2,0,1:T(4,128)(2,1)S(1)} %slice.63), channel_id=1, source_target_pairs={{0,8},{8,16},{16,24},{24,32},{32,40},{40,48},{48,56},{56,64},{64,7... | collective-permute-start | bytes 13832 | tf_op jit(solution)/shard_map/ppermute | solution.py:21
  14.4 6.2 %copy-start.15 = (s32[32]{0:T(128)}, s32[32]{0:T(128)S(1)}, u32[]{:S(2)}) copy-start(s32[32]{0:T(128)S(1)} %multiply_add_fusion) | copy-start | bytes 388
  15.5 5.1 %copy-start.17 = (f32[1,2,2,128]{3,1,2,0:T(2,128)}, f32[1,2,2,128]{3,1,2,0:T(2,128)S(1)}, u32[]{:S(2)}) copy-start(f32[1,2,2,128]{3,1,2,0:T(2,128)S(1)} %copy.197) | copy-start | bytes 6148
  22.2 0.8 copy-start.3
  49.6 4.0 %copy-start.6 = (bf16[256,2048]{1,0:T(8,128)(2,1)S(1)}, bf16[256,2048]{1,0:T(8,128)(2,1)}, u32[]{:S(2)}) copy-start(bf16[256,2048]{1,0:T(8,128)(2,1)} %param.20) | copy-start | bytes 3145732
  50.6 1.3 copy-start.7
  51.9 0.7 copy-start.4
  109.7 2.2 copy-start.11
  109.7 2.3 copy-start.14
  111.9 2.0 copy-start.1
  113.9 79.4 %copy-start.19 = (bf16[1,2048,256]{2,1,0:T(8,128)(2,1)S(1)}, bf16[1,2048,256]{2,1,0:T(8,128)(2,1)}, u32[]{:S(2)}) copy-start(bf16[1,2048,256]{2,1,0:T(8,128)(2,1)} %param.24) | copy-start | bytes 3145732
  190.6 2.6 copy-start.2
  209.2 83.8 %all-to-all-start.1 = ((bf16[32,48,2048]{2,1,0:T(8,128)(2,1)}), bf16[32,48,2048]{2,1,0:T(8,128)(2,1)}, u32[]{:S(2)}, u32[]{:S(2)}) async-start(bf16[32,48,2048]{2,1,0:T(8,128)(2,1)} %convolution_convert_fusion), calls=%async_computation.1 | async-start | bytes 12582912 | tf_op jit(solution)/shard_map/all_to_all | solution.py:302
  217.3 116.3 %reduce-scatter.2.cloned.1.call-start = ((), (), s32[]{:S(2)}) async-start(), calls=%async_computation.3 | async-start | bytes 1179648 | tf_op jit(solution)/shard_map/reduce_scatter | solution.py:310
  298.6 6.6 %copy-start.18 = (f32[1,2,2,128]{3,1,2,0:T(2,128)S(1)}, f32[1,2,2,128]{3,1,2,0:T(2,128)}, u32[]{:S(2)}) copy-start(f32[1,2,2,128]{3,1,2,0:T(2,128)} %copy-done.17) | copy-start | bytes 6148
  299.5 3.0 copy-start.8
  306.3 0.7 copy-start.5
Sparse Core Ops, SparseCore 0:
  298.7 34.8 reduce-scatter.1

commit v2 on v1

--- a/solution.py
+++ b/solution.py
@@ -104,108 +104,396 @@
     return fwd.reshape(heads, size, size), bwd.reshape(heads, size, size)
 
 
-def ring_kernel(n, subs, part, out, right_in, left_in, rs_s, rs_r, ag_s, ag_r):
+def hops(n, half, way):
+    return n // 2 if half == way else n // 2 - 1
+
+
+def streams(n, subs):
+    return [(half, way, sub) for sub in range(subs) for half in range(2) for way in range(2)]
+
+
+def ring_reduce(n, subs, part, land, send_sem, recv_sem, finish):
     me = lax.axis_index("head")
-    right, left = lax.rem(me + 1, n), lax.rem(me + n - 1, n)
-    greet("head", n, me, (1, n - 1))
-    tokens = part.shape[1]
-    piece = tokens // (2 * subs)
-    ways = ((right, 1, right_in), (left, -1, left_in))
-
-    def span(way, sub):
-        return pl.ds((way * subs + sub) * piece, piece)
-
-    def reduce_copy(way, sub, step):
-        peer, sign, land = ways[way]
+    piece = part.shape[1] // (2 * subs)
+    signs = (1, -1)
+
+    def block(half, way, step):
+        return lax.rem(me + signs[way] * (hops(n, half, way) - step) + n, n)
+
+    def span(half, sub):
+        return pl.ds((half * subs + sub) * piece, piece)
+
+    def copy(half, way, sub, step):
         if step == 0:
-            source = part.at[lax.rem(me - sign + n, n), span(way, sub)]
+            source = part.at[block(half, way, 0), span(half, sub)]
         else:
-            source = land.at[step - 1, sub]
+            source = land.at[half, way, sub, step - 1]
         return pltpu.make_async_remote_copy(
             src_ref=source,
-            dst_ref=land.at[step, sub],
-            send_sem=rs_s.at[way, step, sub],
-            recv_sem=rs_r.at[way, step, sub],
-            device_id={"head": peer},
+            dst_ref=land.at[half, way, sub, step],
+            send_sem=send_sem.at[half, way, sub, step],
+            recv_sem=recv_sem.at[half, way, sub, step],
+            device_id={"head": lax.rem(me + signs[way] + n, n)},
             device_id_type=MESH,
         )
 
-    sends = {}
-    for sub in range(subs):
-        for way in range(2):
-            sends[way, sub, 0] = reduce_copy(way, sub, 0)
-            sends[way, sub, 0].start()
-
-    def gather_copy(half, sub, way, step):
-        peer, sign, _ = ways[way]
-        block = lax.rem(me - sign * step + 2 * n, n)
-        view = out.at[block, span(half, sub)]
+    sent = []
+
+    def go(half, way, sub, step):
+        one = copy(half, way, sub, step)
+        one.start()
+        sent.append(one)
+
+    for stream in streams(n, subs):
+        go(*stream, 0)
+    for step in range(n // 2):
+        for half, way, sub in streams(n, subs):
+            last = hops(n, half, way) - 1
+            if step > last:
+                continue
+            copy(half, way, sub, step).wait_recv()
+            if step < last:
+                own = part[block(half, way, step + 1), span(half, sub)]
+                total = land[half, way, sub, step].astype(F32) + own.astype(F32)
+                land[half, way, sub, step] = total.astype(BF)
+                go(half, way, sub, step + 1)
+            elif step == n // 2 - 1:
+                other = land[half, 1 - way, sub, hops(n, half, 1 - way) - 1]
+                total = land[half, way, sub, step].astype(F32) + other.astype(F32)
+                finish(half, sub, span(half, sub), total + part[me, span(half, sub)].astype(F32))
+    return sent
+
+
+def ring_gather(n, subs, out, send_sem, recv_sem):
+    me = lax.axis_index("head")
+    piece = out.shape[1] // (2 * subs)
+    signs = (1, -1)
+    sent = []
+
+    def copy(half, way, sub, step):
+        owner = lax.rem(me - signs[way] * step + n, n)
+        view = out.at[owner, pl.ds((half * subs + sub) * piece, piece)]
         return pltpu.make_async_remote_copy(
             src_ref=view,
             dst_ref=view,
-            send_sem=ag_s.at[half, sub, way, step],
-            recv_sem=ag_r.at[half, sub, way, step],
-            device_id={"head": peer},
+            send_sem=send_sem.at[half, way, sub, step],
+            recv_sem=recv_sem.at[half, way, sub, step],
+            device_id={"head": lax.rem(me + signs[way] + n, n)},
             device_id_type=MESH,
         )
 
-    def hops(half, way):
-        return n // 2 if half == way else n // 2 - 1
-
-    gathers = []
-    for step in range(n - 1):
-        for sub in range(subs):
-            for way in range(2):
-                _, sign, land = ways[way]
-                sends[way, sub, step].wait_recv()
-                block = lax.rem(me - sign * (step + 2) + 2 * n, n)
-                total = land[step, sub].astype(F32) + part[block, span(way, sub)].astype(F32)
-                if step < n - 2:
-                    land[step, sub] = total.astype(BF)
-                    sends[way, sub, step + 1] = reduce_copy(way, sub, step + 1)
-                    sends[way, sub, step + 1].start()
-                else:
-                    out[me, span(way, sub)] = total.astype(BF)
-                    for onward in range(2):
-                        copy = gather_copy(way, sub, onward, 0)
-                        copy.start()
-                        gathers.append(copy)
-    for step in range(n // 2):
-        for sub in range(subs):
-            for half in range(2):
-                for way in range(2):
-                    if step < hops(half, way):
-                        gather_copy(half, sub, way, step).wait_recv()
-                        if step + 1 < hops(half, way):
-                            copy = gather_copy(half, sub, way, step + 1)
-                            copy.start()
-                            gathers.append(copy)
-    for copy in gathers:
+    def go(half, way, sub, step):
+        one = copy(half, way, sub, step)
+        one.start()
+        sent.append(one)
+
+    def relay():
+        for step in range(n // 2):
+            for half, way, sub in streams(n, subs):
+                if step < hops(n, half, way):
+                    arrived = lax.rem(me - signs[way] * (step + 1) + n, n)
+                    view = out.at[arrived, pl.ds((half * subs + sub) * piece, piece)]
+                    pltpu.make_async_remote_copy(
+                        src_ref=view,
+                        dst_ref=view,
+                        send_sem=send_sem.at[half, way, sub, step],
+                        recv_sem=recv_sem.at[half, way, sub, step],
+                        device_id={"head": lax.rem(me + signs[way] + n, n)},
+                        device_id_type=MESH,
+                    ).wait_recv()
+                    if step + 1 < hops(n, half, way):
+                        go(half, way, sub, step + 1)
+
+    return go, relay, sent
+
+
+def layer_kernel(
+    n,
+    n_head,
+    cap,
+    subs,
+    group,
+    part,
+    x_ref,
+    gain_ref,
+    slot_ref,
+    weight_ref,
+    gate_hbm,
+    up_hbm,
+    down_hbm,
+    out_ref,
+    attn,
+    moe_in,
+    pack,
+    batch,
+    result,
+    pair,
+    back,
+    share,
+    gate,
+    up,
+    down,
+    final,
+    land,
+    land2,
+    w_sem,
+    rs_s,
+    rs_r,
+    ag_s,
+    ag_r,
+    fs_s,
+    fs_r,
+    go_s,
+    go_r,
+    zf_s,
+    zf_r,
+    zr_s,
+    zr_r,
+    rt_s,
+    rt_r,
+):
+    me = lax.axis_index("ctx")
+    me_z = lax.axis_index("head")
+    third = cap // 3
+    rows = 2 * third
+    tokens, width = x_ref.shape
+    cols = width // n_head
+    odd = lax.rem(me_z, 2)
+    partner = me_z + 1 - 2 * odd
+
+    loads = [
+        pltpu.make_async_copy(source, target, w_sem.at[i])
+        for i, (source, target) in enumerate(((gate_hbm, gate), (up_hbm, up), (down_hbm, down)))
+    ]
+    for load in loads:
+        load.start()
+
+    barrier = pltpu.get_barrier_semaphore()
+    for r in range(1, n):
+        pl.semaphore_signal(
+            barrier, inc=1, device_id={"ctx": lax.rem(me + r, n)}, device_id_type=MESH
+        )
+    for r in (1, n_head - 1):
+        pl.semaphore_signal(
+            barrier, inc=1, device_id={"head": lax.rem(me_z + r, n_head)}, device_id_type=MESH
+        )
+    pl.semaphore_wait(barrier, n + 1)
+
+    start_gather, relay, gathered = ring_gather(n_head, subs, attn, ag_s, ag_r)
+
+    def keep(half, sub, span, total):
+        attn[me_z, span] = total.astype(BF)
+        for way in range(2):
+            start_gather(half, way, sub, 0)
+
+    reduced = ring_reduce(n_head, subs, part, land, rs_s, rs_r, keep)
+    relay()
+
+    square = jnp.zeros((tokens, 1), F32)
+    for z in range(n_head):
+        resid = x_ref[:, z * cols : (z + 1) * cols].astype(F32) + attn[z].astype(F32)
+        square = square + jnp.sum(resid * resid, axis=-1, keepdims=True)
+    scale = lax.rsqrt(square / width + 1e-06)
+    for z in range(n_head):
+        view = slice(z * cols, (z + 1) * cols)
+        resid = x_ref[:, view].astype(F32) + attn[z].astype(F32)
+        moe_in[:, view] = (resid * scale * gain_ref[:, view]).astype(BF)
+
+    row = lax.broadcasted_iota(jnp.int32, (rows, tokens), 0)
+    row_slot = jnp.where(row < third, row, row + third * odd)
+
+    def send_copy(r):
+        return pltpu.make_async_remote_copy(
+            src_ref=pack.at[r],
+            dst_ref=batch.at[r, pl.ds(0, rows)],
+            send_sem=go_s.at[r],
+            recv_sem=go_r.at[r],
+            device_id={"ctx": lax.rem(me + r, n)},
+            device_id_type=MESH,
+        )
+
+    def forward_copy(g):
+        some = pl.ds(g * group, group)
+        return pltpu.make_async_remote_copy(
+            src_ref=batch.at[some, pl.ds(third, third)],
+            dst_ref=batch.at[some, pl.ds(rows, third)],
+            send_sem=zf_s.at[g],
+            recv_sem=zf_r.at[g],
+            device_id={"head": partner},
+            device_id_type=MESH,
+        )
+
+    def pair_copy(g):
+        some = pl.ds(g * group, group)
+        return pltpu.make_async_remote_copy(
+            src_ref=result.at[some, pl.ds(rows, third)],
+            dst_ref=pair.at[some],
+            send_sem=zr_s.at[g],
+            recv_sem=zr_r.at[g],
+            device_id={"head": partner},
+            device_id_type=MESH,
+        )
+
+    def return_copy(r):
+        return pltpu.make_async_remote_copy(
+            src_ref=result.at[r, pl.ds(0, rows)],
+            dst_ref=back.at[r],
+            send_sem=rt_s.at[r],
+            recv_sem=rt_r.at[r],
+            device_id={"ctx": lax.rem(me - r + n, n)},
+            device_id_type=MESH,
+        )
+
+    def pack_step(step, carry):
+        r = lax.rem(step + 1, n)
+        dest = lax.rem(me + r, n)
+        taken = slot_ref[pl.ds(dest, 1), :] == row_slot
+        share[r] = jnp.where(taken, weight_ref[pl.ds(dest, 1), :], 0.0).astype(BF)
+        pick = jnp.where(taken, 1.0, 0.0).astype(BF)
+        chunk = jnp.dot(pick, moe_in[...], preferred_element_type=F32).astype(BF)
+
+        @pl.when(r > 0)
+        def _():
+            pack[r] = chunk
+            send_copy(r).start()
+
+        @pl.when(r == 0)
+        def _():
+            batch[0, 0:rows] = chunk
+
+        return carry
+
+    lax.fori_loop(0, n, pack_step, 0)
+    for load in loads:
+        load.wait()
+    groups = n // group
+
+    def expert_step(g, carry):
+        @pl.when(g < groups)
+        def _():
+            for i in range(group):
+                r = g * group + i
+
+                @pl.when(r > 0)
+                def _():
+                    send_copy(r).wait_recv()
+
+            forward_copy(g).start()
+
+        @pl.when(jnp.logical_and(g >= 1, g < groups + 1))
+        def _():
+            h = g - 1
+            forward_copy(h).wait_recv()
+            some = pl.ds(h * group, group)
+            token = batch[some].reshape(group * cap, width)
+            gate_val = jnp.dot(token, gate[...], preferred_element_type=F32)
+            up_val = jnp.dot(token, up[...], preferred_element_type=F32)
+            inner = (jax.nn.silu(gate_val) * up_val).astype(BF)
+            y = jnp.dot(inner, down[...], preferred_element_type=F32).astype(BF)
+            result[some] = y.reshape(group, cap, width)
+            pair_copy(h).start()
+
+        @pl.when(g >= 2)
+        def _():
+            h = g - 2
+            pair_copy(h).wait_recv()
+            some = pl.ds(h * group, group)
+            mine = result[some, third:rows].astype(F32) + pair[some].astype(F32)
+            result[some, third:rows] = mine.astype(BF)
+            for i in range(group):
+                r = h * group + i
+
+                @pl.when(r > 0)
+                def _():
+                    return_copy(r).start()
+
+                @pl.when(r == 0)
+                def _():
+                    back[0] = result[0, 0:rows]
+
+        return carry
+
+    lax.fori_loop(0, groups + 2, expert_step, 0)
+
+    def arrive(r, carry):
+        return_copy(r).wait_recv()
+        return carry
+
+    lax.fori_loop(1, n, arrive, 0)
+    shares = share[...].reshape(n * rows, tokens)
+    for z in range(n_head):
+        piece = back[:, :, z * cols : (z + 1) * cols].reshape(n * rows, cols)
+        final[z] = lax.dot_general(
+            shares, piece, (((0,), (0,)), ((), ())), preferred_element_type=F32
+        ).astype(BF)
+
+    mine = pl.ds(pl.multiple_of(me_z * cols, cols), cols)
+
+    def emit(half, sub, span, total):
+        resid = x_ref[span, mine].astype(F32) + attn[me_z, span].astype(F32)
+        out_ref[span] = (resid + total).astype(BF)
+
+    summed = ring_reduce(n_head, subs, final, land2, fs_s, fs_r, emit)
+
+    for copy in reduced + gathered + summed:
         copy.wait_send()
-    for copy in sends.values():
-        copy.wait_send()
-
-
-def ring_sum(part, subs=2):
-    n, tokens, cols = part.shape
+
+    def drain(r, carry):
+        send_copy(r).wait_send()
+        return_copy(r).wait_send()
+        return carry
+
+    lax.fori_loop(1, n, drain, 0)
+
+    def drain_pairs(g, carry):
+        forward_copy(g).wait_send()
+        pair_copy(g).wait_send()
+        return carry
+
+    lax.fori_loop(0, groups, drain_pairs, 0)
+
+
+def layer_tail(part, x, gain, slot, weight, w_gate, w_up, w_down, n, cap, subs=2, group=4):
+    n_head, tokens, cols = part.shape
+    width = n_head * cols
+    rows = 2 * cap // 3
+    ffd = w_gate.shape[1]
     piece = tokens // (2 * subs)
     vmem = pl.BlockSpec(memory_space=pltpu.VMEM)
+    hbm = pl.BlockSpec(memory_space=pl.ANY)
+    dma = pltpu.SemaphoreType.DMA
+    ring = dma((2, 2, subs, n_head // 2))
     return pl.pallas_call(
-        functools.partial(ring_kernel, n, subs),
-        out_shape=jax.ShapeDtypeStruct(part.shape, BF),
-        in_specs=[vmem],
+        functools.partial(layer_kernel, n, n_head, cap, subs, group),
+        out_shape=jax.ShapeDtypeStruct((tokens, cols), BF),
+        in_specs=[vmem] * 5 + [hbm] * 3,
         out_specs=vmem,
         scratch_shapes=[
-            pltpu.VMEM((n - 1, subs, piece, cols), BF),
-            pltpu.VMEM((n - 1, subs, piece, cols), BF),
-            pltpu.SemaphoreType.DMA((2, n - 1, subs)),
-            pltpu.SemaphoreType.DMA((2, n - 1, subs)),
-            pltpu.SemaphoreType.DMA((2, subs, 2, n // 2)),
-            pltpu.SemaphoreType.DMA((2, subs, 2, n // 2)),
-        ],
-        compiler_params=pltpu.CompilerParams(collective_id=2, has_side_effects=True),
-        name="ring_sum",
-    )(part)
+            pltpu.VMEM((n_head, tokens, cols), BF),
+            pltpu.VMEM((tokens, width), BF),
+            pltpu.VMEM((n, rows, width), BF),
+            pltpu.VMEM((n, cap, width), BF),
+            pltpu.VMEM((n, cap, width), BF),
+            pltpu.VMEM((n, cap // 3, width), BF),
+            pltpu.VMEM((n, rows, width), BF),
+            pltpu.VMEM((n, rows, tokens), BF),
+            pltpu.VMEM((width, ffd), BF),
+            pltpu.VMEM((width, ffd), BF),
+            pltpu.VMEM((ffd, width), BF),
+            pltpu.VMEM((n_head, tokens, cols), BF),
+            pltpu.VMEM((2, 2, subs, n_head // 2, piece, cols), BF),
+            pltpu.VMEM((2, 2, subs, n_head // 2, piece, cols), BF),
+            dma((3,)),
+        ]
+        + [ring] * 6
+        + [dma((n,))] * 2
+        + [dma((n // group,))] * 4
+        + [dma((n,))] * 2,
+        compiler_params=pltpu.CompilerParams(
+            collective_id=2, has_side_effects=True, vmem_limit_bytes=58 << 20
+        ),
+        name="layer_tail",
+    )(part, x, gain.reshape(1, width), slot, weight, w_gate, w_up, w_down)
 
 
 def mm(spec, a, b):
@@ -272,16 +560,10 @@
     attended = mm("hts,shd->thd", scores, vals) + mm("thd,hde->the", queries, state_in) * lead
     headed = rms_norm(attended, norm_gain.reshape(heads_here, head_size)).reshape(tok_dev, chans)
     partial_out = mm("ti,izc->ztc", headed, w_out.reshape(chans, n_head, cols)).astype(BF)
-    attn_total = ring_sum(partial_out)
-
     dov = (mm("thd,shd->hts", cots, vals) * decay_mask).astype(BF)
     grad_q = mm("hts,shd->thd", dov, keys) + lead * mm("the,hde->thd", cots, state_in)
     grad_k = mm("hts,thd->shd", dov, queries) + tail * mm("the,hde->thd", vals, grad_in)
     grad_v = mm("hts,the->she", scores, cots) + tail * mm("thd,hde->the", keys, grad_in)
-
-    resid_full = x_float + attn_total.transpose(1, 0, 2).reshape(tok_dev, width).astype(F32)
-    moe_in = rms_norm(resid_full, gain_moe).astype(BF)
-    resid_mine = lax.dynamic_slice_in_dim(resid_full, my_head * cols, cols, 1)
 
     wanted = EXP_CTX * jnp.arange(n_ctx, dtype=jnp.int32)[:, None] + local_expert
     chosen = expert_ids.T[:, None, :] == wanted[None]
@@ -290,27 +572,18 @@
     ranks = mm("et,tu->eu", hot.astype(BF), earlier).astype(jnp.int32)
     slot = jnp.where(hot, ranks, -1)
     weight = jnp.sum(jnp.where(chosen, route_weights.T[:, None, :], 0.0), axis=0)
-    taken = slot[:, None, :] == jnp.arange(cap, dtype=jnp.int32)[None, :, None]
-    pick = taken.astype(BF)
-    share = jnp.where(taken, weight[:, None, :], 0.0).astype(BF)
-
-    buffer = mm("ost,td->osd", pick, moe_in).astype(BF)
-    batch = lax.all_to_all(buffer, "ctx", split_axis=0, concat_axis=0, tiled=True)
-    gate_val = jnp.einsum("ncd,df->ncf", batch, w_gate[0], preferred_element_type=F32)
-    up_val = jnp.einsum("ncd,df->ncf", batch, w_up[0], preferred_element_type=F32)
-    inner = (jax.nn.silu(gate_val) * up_val).astype(BF)
-    returned = lax.all_to_all(
-        jnp.einsum("ncf,fd->ncd", inner, w_down[0], preferred_element_type=F32).astype(BF),
-        "ctx",
-        split_axis=0,
-        concat_axis=0,
-        tiled=True,
+    layer_out = layer_tail(
+        partial_out,
+        hidden_in,
+        gain_moe,
+        slot,
+        weight,
+        w_gate[0],
+        w_up[0],
+        w_down[0],
+        n_ctx,
+        cap,
     )
-    total = mm("ost,osd->td", share, returned)
-    moe_out = lax.psum_scatter(total.astype(BF), "head", scatter_dimension=1, tiled=True).astype(
-        F32
-    )
-    layer_out = (resid_mine + moe_out).astype(BF)
     return (
         layer_out,
         grad_q.reshape(tok_dev, chans).astype(BF),

time: 343 us -> 252 us (0.73)
  Pallas kernels: 67.3 us -> 210 us
  waiting for transfers between devices: 95.9 us -> 0.01 us
  blocking collectives: 76.7 us -> 0 us
  matrix products: 39.3 us -> 17.8 us
  between operations: 14.4 us -> 0.9 us
  local copies, waits for them, and re-layouts: 19.4 us -> 10.2 us
  other arithmetic: 19 us -> 10 us
  starting transfers between devices: 10.1 us -> 1.91 us
    pallas_call x1, Pallas kernels: 46.1 us -> 189 us  [layer_tail(): pl.pallas_call(functools.partial(layer_kernel, n, n_head, cap, subs, grou...]
    all_to_all x1 -> x0, blocking collectives: 76.7 us -> none  [body(): lax.all_to_all(buffer, 'ctx', split_axis=0, concat_axis=0, tiled=True)]
    all_to_all x1 -> x0, waiting for transfers between devices: 74.2 us -> none  [body(): lax.all_to_all(jnp.einsum('ncf,fd->ncd', inner, w_down[0], preferred_elem...]
    reduce_scatter x1 -> x0, waiting for transfers between devices: 21.7 us -> none  [body(): lax.psum_scatter(total.astype(BF), 'head', scatter_dimension=1, tiled=True)]
    dot_general x2 -> x0, matrix products: 15.9 us -> none  [the longest x1 12.8 us: body(): jnp.einsum('ncf,fd->ncd', inner, w_down[0], preferred_element_type=F32)]
    all_to_all x1 -> x0, starting transfers between devices: 8.12 us -> none  [body(): lax.all_to_all(jnp.einsum('ncf,fd->ncd', inner, w_down[0], preferred_elem...]
    convert_element_type x2 -> x0, local copies, waits for them, and re-layouts: 5.82 us -> none  [body(): attn_total.transpose(1, 0, 2).reshape(tok_dev, width).astype(F32)]
    dot_general x16 -> x14, matrix products: 21.1 us -> 15.4 us  [mm(): jnp.einsum(spec, a.astype(BF), b.astype(BF), preferred_element_type=F32)]
  transfers between devices with their start and end apart: 3 -> 1, of which waited for: 2 -> 0; matrix products, arithmetic and copies ran while one was open for 5% -> 2% of each run, Pallas kernels for 0% -> 0%
where the time goes in v2:
time: 252 us; the launch traced here: 251 us
  Pallas kernels  210 us (83%)
  matrix products  17.8 us (7%)
  local copies, waits for them, and re-layouts  10.2 us (4%)
  other arithmetic  10 us (4%)
    pallas_call x1, Pallas kernels, layer_tail(): pl.pallas_call(functools.partial(layer_kernel, n, n_head, cap, subs, grou...  189 us
    pallas_call x1, Pallas kernels, state_exchange(): pl.pallas_call(functools.partial(state_kernel, n, rows), out_shape=(out,...  21.2 us
    dot_general x14, matrix products, mm(): jnp.einsum(spec, a.astype(BF), b.astype(BF), preferred_element_type=F32)  15.4 us
    unnamed x31, local copies, waits for them, and re-layouts  6.07 us
  transfers between devices with their start and end apart: 1, of which 0 were waited for; matrix products, arithmetic and copies ran while one was open for 2% of the time, Pallas kernels for 0%

profile of v2, /device:TPU:10, one launch (start us, length us, event | category | flops | bytes accessed | tf_op | source)
XLA Modules:
  0.0 251.0 jit_solution(3093734557064122713)
XLA Ops:
  0.6 1.7 fusion
  2.9 2.3 convolution_convert_fusion.1
  5.9 1.9 collective-permute-start
  11.7 1.1 maximum_convert_fusion
  12.8 1.4 fusion.41
  14.9 0.9 convert_element_type.102
  16.6 1.6 fusion.29
  18.3 1.0 copy.156
  19.3 1.1 fusion.30
  21.4 21.2 %state_exchange.1 = (f32[32,8,128]{2,1,0:T(8,128)}, f32[32,8,128]{2,1,0:T(8,128)}) custom-call(f32[32,24,128]{2,1,0:T(8,128)} %pad_maximum_fusion.give), custom_call_target="tpu_custom_call" | custom-call | tf_op jit(solution)/shard_map/state_exchange/pallas_call | solution.py:90
  42.7 1.0 convert_element_type.118
  43.6 1.1 fusion.11
  44.7 0.9 fusion.12
  45.6 1.2 fusion.5
  46.9 1.0 fusion.6
  47.9 0.9 fusion.13
  48.8 0.9 fusion.14
  50.6 1.7 copy.146
  52.3 1.2 fusion.16
  54.2 1.3 fusion.15
  56.3 1.3 multiply_reduce_fusion
  57.7 2.7 %fusion.3.part = bf16[8,256,256]{2,1,0:T(8,128)(2,1)} fusion(bf16[256,256,1]{0,1,2:T(8,128)(2,1)S(1)} %bitcast.136, bf16[32,8,8,256]{3,2,1,0:T(8,128)(2,1)} %bitcast.128), kind=kOutput, calls=%fused_computation.6 | convolution fusion | flops 268959744 | bytes 2228224 | tf_op jit(solution)/shard_map/ti,izc->ztc/dot_general | solution.py:500
  60.4 189.0 %layer_tail.1 = bf16[256,256]{1,0:T(8,128)(2,1)} custom-call(bf16[8,256,256]{2,1,0:T(8,128)(2,1)} %fusion.3.part, bf16[256,2048]{1,0:T(8,128)(2,1)} %x_ref.1, f32[1,2048]{1,0:T(1,128)} %bitcast.144, s32[32,256]{1,0:T(8,128)} %fusion.18.slot_ref, f32[32,256]{1,0:T(8,128)} %fusion.28.weight_ref, bf16[2048,256]{1,0:T(8,128)(2,1)} %bitcast.129, ...), custom_call_target="tpu_custom_call" | custom-call | tf_op jit(solution)/shard_map/layer_tail/pallas_call | solution.py:466
  249.5 1.6 copy.191
  (59 shorter events, 10.1 us)
Async XLA Ops:
  0.6 2.2 copy-start
  2.8 5.0 %copy-start.8 = (f32[4,3,256]{2,0,1:T(4,128)S(1)}, f32[4,3,256]{2,0,1:T(4,128)}, u32[]{:S(2)}) copy-start(f32[4,3,256]{2,0,1:T(4,128)} %param.17) | copy-start | bytes 36868
  2.8 5.1 %copy-start.10 = (f32[256,2]{0,1:T(2,128)S(1)}, f32[256,2]{0,1:T(2,128)}, u32[]{:S(2)}) copy-start(f32[256,2]{0,1:T(2,128)} %param.18) | copy-start | bytes 6148
  2.8 6.4 %copy-start.7 = (s32[256,8]{0,1:T(8,128)S(1)}, s32[256,8]{0,1:T(8,128)}, u32[]{:S(2)}) copy-start(s32[256,8]{0,1:T(8,128)} %param.22) | copy-start | bytes 24580
  2.8 7.3 %copy-start.9 = (f32[256,8]{0,1:T(8,128)S(1)}, f32[256,8]{0,1:T(8,128)}, u32[]{:S(2)}) copy-start(f32[256,8]{0,1:T(8,128)} %param.23) | copy-start | bytes 24580
  2.9 8.6 %copy-start.5 = (bf16[256,256]{1,0:T(8,128)(2,1)S(1)}, bf16[256,256]{1,0:T(8,128)(2,1)}, u32[]{:S(2)}) copy-start(bf16[256,256]{1,0:T(8,128)(2,1)} %param.27) | copy-start | bytes 393220
  5.2 0.7 copy-start.3
  5.9 5.8 %collective-permute-start = (bf16[3,3,256]{2,0,1:T(4,128)(2,1)S(1)}, bf16[3,3,256]{2,0,1:T(4,128)(2,1)S(1)}, u32[]{:S(2)}, u32[]{:S(2)}) collective-permute-start(bf16[3,3,256]{2,0,1:T(4,128)(2,1)S(1)} %slice.63), channel_id=1, source_target_pairs={{0,8},{8,16},{16,24},{24,32},{32,40},{40,48},{48,56},{56,64},{64,7... | collective-permute-start | bytes 13832 | tf_op jit(solution)/shard_map/ppermute | solution.py:21
  15.8 0.8 copy-start.1
  42.6 4.2 %copy-start.6 = (pred[256,256]{1,0:T(8,128)(4,1)S(1)}, pred[256,256]{1,0:T(8,128)(4,1)}, u32[]{:S(2)}) copy-start(pred[256,256]{1,0:T(8,128)(4,1)} %iota_compare_fusion.1) | copy-start | bytes 196612
  42.6 5.3 %copy-start.4 = (f32[32,8,128]{2,1,0:T(8,128)S(1)}, f32[32,8,128]{2,1,0:T(8,128)}, u32[]{:S(2)}) copy-start(f32[32,8,128]{2,1,0:T(8,128)} %get-tuple-element.6) | copy-start | bytes 393220
  46.9 3.7 %copy-start.2 = (bf16[2,256,256]{2,1,0:T(8,128)(2,1)}, bf16[2,256,256]{2,1,0:T(8,128)(2,1)S(1)}, u32[]{:S(2)}) copy-start(bf16[2,256,256]{2,1,0:T(8,128)(2,1)S(1)} %fusion.5) | copy-start | bytes 786436
  49.7 7.9 %copy-start.11 = (f32[256]{0:T(256)S(1)}, f32[256]{0:T(256)}, u32[]{:S(2)}) copy-start(f32[256]{0:T(256)} %param.19) | copy-start | bytes 3076

commit v3 on v2

--- a/solution.py
+++ b/solution.py
@@ -299,24 +299,29 @@
         resid = x_ref[:, view].astype(F32) + attn[z].astype(F32)
         moe_in[:, view] = (resid * scale * gain_ref[:, view]).astype(BF)
 
-    row = lax.broadcasted_iota(jnp.int32, (rows, tokens), 0)
-    row_slot = jnp.where(row < third, row, row + third * odd)
-
-    def send_copy(r):
+    row = lax.broadcasted_iota(jnp.int32, (third, tokens), 0)
+    row_slots = (row, row + third * (1 + odd))
+    groups = n // group
+
+    def distance(g, i):
+        return g + i * groups
+
+    def send_copy(part_index, g, i):
+        place = g * group + i
         return pltpu.make_async_remote_copy(
-            src_ref=pack.at[r],
-            dst_ref=batch.at[r, pl.ds(0, rows)],
-            send_sem=go_s.at[r],
-            recv_sem=go_r.at[r],
-            device_id={"ctx": lax.rem(me + r, n)},
+            src_ref=pack.at[part_index, place],
+            dst_ref=batch.at[part_index, place],
+            send_sem=go_s.at[part_index, place],
+            recv_sem=go_r.at[part_index, place],
+            device_id={"ctx": lax.rem(me + distance(g, i), n)},
             device_id_type=MESH,
         )
 
     def forward_copy(g):
         some = pl.ds(g * group, group)
         return pltpu.make_async_remote_copy(
-            src_ref=batch.at[some, pl.ds(third, third)],
-            dst_ref=batch.at[some, pl.ds(rows, third)],
+            src_ref=batch.at[1, some],
+            dst_ref=batch.at[2, some],
             send_sem=zf_s.at[g],
             recv_sem=zf_r.at[g],
             device_id={"head": partner},
@@ -326,7 +331,7 @@
     def pair_copy(g):
         some = pl.ds(g * group, group)
         return pltpu.make_async_remote_copy(
-            src_ref=result.at[some, pl.ds(rows, third)],
+            src_ref=result.at[2, some],
             dst_ref=pair.at[some],
             send_sem=zr_s.at[g],
             recv_sem=zr_r.at[g],
@@ -334,95 +339,104 @@
             device_id_type=MESH,
         )
 
-    def return_copy(r):
+    def return_copy(part_index, g, i):
+        place = g * group + i
         return pltpu.make_async_remote_copy(
-            src_ref=result.at[r, pl.ds(0, rows)],
-            dst_ref=back.at[r],
-            send_sem=rt_s.at[r],
-            recv_sem=rt_r.at[r],
-            device_id={"ctx": lax.rem(me - r + n, n)},
+            src_ref=result.at[part_index, place],
+            dst_ref=back.at[part_index, place],
+            send_sem=rt_s.at[part_index, place],
+            recv_sem=rt_r.at[part_index, place],
+            device_id={"ctx": lax.rem(me - distance(g, i) + n, n)},
             device_id_type=MESH,
         )
 
-    def pack_step(step, carry):
-        r = lax.rem(step + 1, n)
-        dest = lax.rem(me + r, n)
-        taken = slot_ref[pl.ds(dest, 1), :] == row_slot
-        share[r] = jnp.where(taken, weight_ref[pl.ds(dest, 1), :], 0.0).astype(BF)
-        pick = jnp.where(taken, 1.0, 0.0).astype(BF)
-        chunk = jnp.dot(pick, moe_in[...], preferred_element_type=F32).astype(BF)
-
-        @pl.when(r > 0)
+    def each(g, act):
+        @pl.when(g > 0)
         def _():
-            pack[r] = chunk
-            send_copy(r).start()
-
-        @pl.when(r == 0)
-        def _():
-            batch[0, 0:rows] = chunk
-
+            act(g, 0)
+
+        for i in range(1, group):
+            act(g, i)
+
+    for part_index in (1, 0):
+
+        def pack_step(g, carry, part_index=part_index):
+            picks = []
+            for i in range(group):
+                dest = lax.rem(me + distance(g, i), n)
+                taken = slot_ref[pl.ds(dest, 1), :] == row_slots[part_index]
+                chosen = jnp.where(taken, weight_ref[pl.ds(dest, 1), :], 0.0)
+                share[part_index, g * group + i] = chosen.astype(BF)
+                picks.append(jnp.where(taken, 1.0, 0.0).astype(BF))
+            chunk = jnp.dot(
+                jnp.concatenate(picks, axis=0), moe_in[...], preferred_element_type=F32
+            ).astype(BF)
+            for i in range(group):
+                pack[part_index, g * group + i] = chunk[i * third : (i + 1) * third]
+            each(g, lambda g, i: send_copy(part_index, g, i).start())
+
+            @pl.when(g == 0)
+            def _():
+                batch[part_index, 0] = chunk[0:third]
+
+            return carry
+
+        lax.fori_loop(0, groups, pack_step, 0)
+
+    def forward_step(g, carry):
+        each(g, lambda g, i: send_copy(1, g, i).wait_recv())
+        forward_copy(g).start()
         return carry
 
-    lax.fori_loop(0, n, pack_step, 0)
+    lax.fori_loop(0, groups, forward_step, 0)
     for load in loads:
         load.wait()
-    groups = n // group
 
     def expert_step(g, carry):
         @pl.when(g < groups)
         def _():
-            for i in range(group):
-                r = g * group + i
-
-                @pl.when(r > 0)
-                def _():
-                    send_copy(r).wait_recv()
-
-            forward_copy(g).start()
-
-        @pl.when(jnp.logical_and(g >= 1, g < groups + 1))
-        def _():
-            h = g - 1
-            forward_copy(h).wait_recv()
-            some = pl.ds(h * group, group)
-            token = batch[some].reshape(group * cap, width)
+            each(g, lambda g, i: send_copy(0, g, i).wait_recv())
+            forward_copy(g).wait_recv()
+            some = pl.ds(g * group, group)
+            token = batch[:, some].reshape(group * cap, width)
             gate_val = jnp.dot(token, gate[...], preferred_element_type=F32)
             up_val = jnp.dot(token, up[...], preferred_element_type=F32)
             inner = (jax.nn.silu(gate_val) * up_val).astype(BF)
             y = jnp.dot(inner, down[...], preferred_element_type=F32).astype(BF)
-            result[some] = y.reshape(group, cap, width)
-            pair_copy(h).start()
+            result[:, some] = y.reshape(3, group, third, width)
+            pair_copy(g).start()
+            each(g, lambda g, i: return_copy(0, g, i).start())
+
+        @pl.when(g == 0)
+        def _():
+            back[0, 0] = result[0, 0]
 
         @pl.when(g >= 2)
         def _():
             h = g - 2
             pair_copy(h).wait_recv()
             some = pl.ds(h * group, group)
-            mine = result[some, third:rows].astype(F32) + pair[some].astype(F32)
-            result[some, third:rows] = mine.astype(BF)
-            for i in range(group):
-                r = h * group + i
-
-                @pl.when(r > 0)
-                def _():
-                    return_copy(r).start()
-
-                @pl.when(r == 0)
-                def _():
-                    back[0] = result[0, 0:rows]
+            mine = result[1, some].astype(F32) + pair[some].astype(F32)
+            result[1, some] = mine.astype(BF)
+            each(h, lambda h, i: return_copy(1, h, i).start())
+
+        @pl.when(g == 2)
+        def _():
+            back[1, 0] = result[1, 0]
 
         return carry
 
     lax.fori_loop(0, groups + 2, expert_step, 0)
 
-    def arrive(r, carry):
-        return_copy(r).wait_recv()
+    def arrive(g, carry):
+        for part_index in range(2):
+            each(g, lambda g, i: return_copy(part_index, g, i).wait_recv())
         return carry
 
-    lax.fori_loop(1, n, arrive, 0)
+    lax.fori_loop(0, groups, arrive, 0)
     shares = share[...].reshape(n * rows, tokens)
     for z in range(n_head):
-        piece = back[:, :, z * cols : (z + 1) * cols].reshape(n * rows, cols)
+        piece = back[:, :, :, z * cols : (z + 1) * cols].reshape(n * rows, cols)
         final[z] = lax.dot_general(
             shares, piece, (((0,), (0,)), ((), ())), preferred_element_type=F32
         ).astype(BF)
@@ -438,25 +452,21 @@
     for copy in reduced + gathered + summed:
         copy.wait_send()
 
-    def drain(r, carry):
-        send_copy(r).wait_send()
-        return_copy(r).wait_send()
-        return carry
-
-    lax.fori_loop(1, n, drain, 0)
-
-    def drain_pairs(g, carry):
+    def drain(g, carry):
+        for part_index in range(2):
+            each(g, lambda g, i: send_copy(part_index, g, i).wait_send())
+            each(g, lambda g, i: return_copy(part_index, g, i).wait_send())
         forward_copy(g).wait_send()
         pair_copy(g).wait_send()
         return carry
 
-    lax.fori_loop(0, groups, drain_pairs, 0)
+    lax.fori_loop(0, groups, drain, 0)
 
 
 def layer_tail(part, x, gain, slot, weight, w_gate, w_up, w_down, n, cap, subs=2, group=4):
     n_head, tokens, cols = part.shape
     width = n_head * cols
-    rows = 2 * cap // 3
+    third = cap // 3
     ffd = w_gate.shape[1]
     piece = tokens // (2 * subs)
     vmem = pl.BlockSpec(memory_space=pltpu.VMEM)
@@ -471,12 +481,12 @@
         scratch_shapes=[
             pltpu.VMEM((n_head, tokens, cols), BF),
             pltpu.VMEM((tokens, width), BF),
-            pltpu.VMEM((n, rows, width), BF),
-            pltpu.VMEM((n, cap, width), BF),
-            pltpu.VMEM((n, cap, width), BF),
-            pltpu.VMEM((n, cap // 3, width), BF),
-            pltpu.VMEM((n, rows, width), BF),
-            pltpu.VMEM((n, rows, tokens), BF),
+            pltpu.VMEM((2, n, third, width), BF),
+            pltpu.VMEM((3, n, third, width), BF),
+            pltpu.VMEM((3, n, third, width), BF),
+            pltpu.VMEM((n, third, width), BF),
+            pltpu.VMEM((2, n, third, width), BF),
+            pltpu.VMEM((2, n, third, tokens), BF),
             pltpu.VMEM((width, ffd), BF),
             pltpu.VMEM((width, ffd), BF),
             pltpu.VMEM((ffd, width), BF),
@@ -486,9 +496,9 @@
             dma((3,)),
         ]
         + [ring] * 6
-        + [dma((n,))] * 2
+        + [dma((2, n))] * 2
         + [dma((n // group,))] * 4
-        + [dma((n,))] * 2,
+        + [dma((2, n))] * 2,
         compiler_params=pltpu.CompilerParams(
             collective_id=2, has_side_effects=True, vmem_limit_bytes=58 << 20
         ),

time: 252 us -> 244 us (0.968)
  Pallas kernels: 210 us -> 202 us
    pallas_call x1, Pallas kernels: 189 us -> 181 us  [layer_tail(): pl.pallas_call(functools.partial(layer_kernel, n, n_head, cap, subs, grou...]
where the time goes in v3:
time: 244 us; the launch traced here: 243 us
  Pallas kernels  202 us (83%)
  matrix products  17.8 us (7%)
  local copies, waits for them, and re-layouts  10.2 us (4%)
  other arithmetic  10 us (4%)
    pallas_call x1, Pallas kernels, layer_tail(): pl.pallas_call(functools.partial(layer_kernel, n, n_head, cap, subs, grou...  181 us
    pallas_call x1, Pallas kernels, state_exchange(): pl.pallas_call(functools.partial(state_kernel, n, rows), out_shape=(out,...  21.2 us
    dot_general x14, matrix products, mm(): jnp.einsum(spec, a.astype(BF), b.astype(BF), preferred_element_type=F32)  15.4 us
    unnamed x31, local copies, waits for them, and re-layouts  6.07 us
  transfers between devices with their start and end apart: 1, of which 0 were waited for; matrix products, arithmetic and copies ran while one was open for 2% of the time, Pallas kernels for 0%

profile of v3, /device:TPU:10, one launch (start us, length us, event | category | flops | bytes accessed | tf_op | source)
XLA Modules:
  0.0 243.0 jit_solution(15185663247803879690)
XLA Ops:
  0.6 1.7 fusion
  2.9 2.3 convolution_convert_fusion.1
  5.9 1.9 collective-permute-start
  11.7 1.1 maximum_convert_fusion
  12.8 1.4 fusion.41
  14.9 0.9 convert_element_type.102
  16.6 1.6 fusion.29
  18.3 1.0 copy.156
  19.3 1.1 fusion.30
  21.4 21.2 %state_exchange.1 = (f32[32,8,128]{2,1,0:T(8,128)}, f32[32,8,128]{2,1,0:T(8,128)}) custom-call(f32[32,24,128]{2,1,0:T(8,128)} %pad_maximum_fusion.give), custom_call_target="tpu_custom_call" | custom-call | tf_op jit(solution)/shard_map/state_exchange/pallas_call | solution.py:90
  42.7 1.0 convert_element_type.118
  43.6 1.1 fusion.11
  44.7 0.9 fusion.12
  45.6 1.2 fusion.5
  46.9 1.0 fusion.6
  47.9 0.9 fusion.13
  48.8 0.9 fusion.14
  50.6 1.7 copy.146
  52.3 1.2 fusion.16
  54.2 1.3 fusion.15
  56.3 1.3 multiply_reduce_fusion
  57.7 2.7 %fusion.3.part = bf16[8,256,256]{2,1,0:T(8,128)(2,1)} fusion(bf16[256,256,1]{0,1,2:T(8,128)(2,1)S(1)} %bitcast.136, bf16[32,8,8,256]{3,2,1,0:T(8,128)(2,1)} %bitcast.128), kind=kOutput, calls=%fused_computation.6 | convolution fusion | flops 268959744 | bytes 2228224 | tf_op jit(solution)/shard_map/ti,izc->ztc/dot_general | solution.py:510
  60.4 181.0 %layer_tail.1 = bf16[256,256]{1,0:T(8,128)(2,1)} custom-call(bf16[8,256,256]{2,1,0:T(8,128)(2,1)} %fusion.3.part, bf16[256,2048]{1,0:T(8,128)(2,1)} %x_ref.1, f32[1,2048]{1,0:T(1,128)} %bitcast.144, s32[32,256]{1,0:T(8,128)} %fusion.18.slot_ref, f32[32,256]{1,0:T(8,128)} %fusion.28.weight_ref, bf16[2048,256]{1,0:T(8,128)(2,1)} %bitcast.129, ...), custom_call_target="tpu_custom_call" | custom-call | tf_op jit(solution)/shard_map/layer_tail/pallas_call | solution.py:476
  241.4 1.6 copy.191
  (59 shorter events, 10.1 us)
Async XLA Ops:
  0.6 2.2 copy-start
  2.8 5.0 %copy-start.8 = (f32[4,3,256]{2,0,1:T(4,128)S(1)}, f32[4,3,256]{2,0,1:T(4,128)}, u32[]{:S(2)}) copy-start(f32[4,3,256]{2,0,1:T(4,128)} %param.17) | copy-start | bytes 36868
  2.8 5.1 %copy-start.10 = (f32[256,2]{0,1:T(2,128)S(1)}, f32[256,2]{0,1:T(2,128)}, u32[]{:S(2)}) copy-start(f32[256,2]{0,1:T(2,128)} %param.18) | copy-start | bytes 6148
  2.8 6.4 %copy-start.7 = (s32[256,8]{0,1:T(8,128)S(1)}, s32[256,8]{0,1:T(8,128)}, u32[]{:S(2)}) copy-start(s32[256,8]{0,1:T(8,128)} %param.22) | copy-start | bytes 24580
  2.8 7.3 %copy-start.9 = (f32[256,8]{0,1:T(8,128)S(1)}, f32[256,8]{0,1:T(8,128)}, u32[]{:S(2)}) copy-start(f32[256,8]{0,1:T(8,128)} %param.23) | copy-start | bytes 24580
  2.9 8.6 %copy-start.5 = (bf16[256,256]{1,0:T(8,128)(2,1)S(1)}, bf16[256,256]{1,0:T(8,128)(2,1)}, u32[]{:S(2)}) copy-start(bf16[256,256]{1,0:T(8,128)(2,1)} %param.27) | copy-start | bytes 393220
  5.2 0.7 copy-start.3
  5.9 5.8 %collective-permute-start = (bf16[3,3,256]{2,0,1:T(4,128)(2,1)S(1)}, bf16[3,3,256]{2,0,1:T(4,128)(2,1)S(1)}, u32[]{:S(2)}, u32[]{:S(2)}) collective-permute-start(bf16[3,3,256]{2,0,1:T(4,128)(2,1)S(1)} %slice.63), channel_id=1, source_target_pairs={{0,8},{8,16},{16,24},{24,32},{32,40},{40,48},{48,56},{56,64},{64,7... | collective-permute-start | bytes 13832 | tf_op jit(solution)/shard_map/ppermute | solution.py:21
  15.8 0.8 copy-start.1
  42.6 4.2 %copy-start.6 = (pred[256,256]{1,0:T(8,128)(4,1)S(1)}, pred[256,256]{1,0:T(8,128)(4,1)}, u32[]{:S(2)}) copy-start(pred[256,256]{1,0:T(8,128)(4,1)} %iota_compare_fusion.1) | copy-start | bytes 196612
  42.6 5.3 %copy-start.4 = (f32[32,8,128]{2,1,0:T(8,128)S(1)}, f32[32,8,128]{2,1,0:T(8,128)}, u32[]{:S(2)}) copy-start(f32[32,8,128]{2,1,0:T(8,128)} %get-tuple-element.6) | copy-start | bytes 393220
  46.9 3.7 %copy-start.2 = (bf16[2,256,256]{2,1,0:T(8,128)(2,1)}, bf16[2,256,256]{2,1,0:T(8,128)(2,1)S(1)}, u32[]{:S(2)}) copy-start(bf16[2,256,256]{2,1,0:T(8,128)(2,1)S(1)} %fusion.5) | copy-start | bytes 786436
  49.7 7.9 %copy-start.11 = (f32[256]{0:T(256)S(1)}, f32[256]{0:T(256)}, u32[]{:S(2)}) copy-start(f32[256]{0:T(256)} %param.19) | copy-start | bytes 3076

commit v4 on v3

--- a/solution.py
+++ b/solution.py
@@ -34,8 +34,42 @@
     pl.semaphore_wait(barrier, len(offsets))
 
 
-def state_kernel(n, rows, give, fwd_out, bwd_out, got, back, land, s1, r1, s2, r2):
+def contract(a, b, left, right):
+    return lax.dot_general(
+        a.astype(BF), b.astype(BF), (((left,), (right,)), ((), ())), preferred_element_type=F32
+    )
+
+
+def core_kernel(
+    n,
+    heads,
+    q,
+    k,
+    v,
+    do,
+    cum_col,
+    cum_row,
+    gain,
+    w_out,
+    part,
+    grad_q,
+    grad_k,
+    grad_v,
+    intra,
+    give,
+    got,
+    back,
+    land,
+    s1,
+    r1,
+    s2,
+    r2,
+):
     me = lax.axis_index("ctx")
+    tokens, chans = q.shape
+    size = chans // heads
+    per = n // heads
+    rows = size // per
     greet("ctx", n, me, range(1, n))
 
     def push(source, target, send_sem, recv_sem, r):
@@ -49,59 +83,108 @@
             device_id_type=MESH,
         )
 
+    def view(h):
+        return slice(h * size, (h + 1) * size)
+
+    def factors(h):
+        cum = cum_col[:, h : h + 1]
+        total = cum_row[h : h + 1, tokens - 1 : tokens]
+        return jnp.exp(cum), jnp.exp(total - cum), jnp.exp(total)
+
+    for h in range(heads):
+        lead, tail, decay = factors(h)
+        some = slice(h * per, (h + 1) * per)
+        summary = contract(k[:, view(h)].astype(F32) * tail, v[:, view(h)], 0, 0)
+        backsum = contract(q[:, view(h)].astype(F32) * lead, do[:, view(h)], 0, 0)
+        give[some, 0:rows] = summary.reshape(per, rows, size)
+        give[some, rows : 2 * rows] = backsum.reshape(per, rows, size)
+        give[some, 2 * rows : 3 * rows] = jnp.broadcast_to(
+            decay.reshape(1, 1, 1), (per, rows, size)
+        )
     first = [push(give, got, s1, r1, r) for r in range(1, n)]
     for copy in first:
         copy.start()
     got[me] = give[me]
+
+    t_index = lax.broadcasted_iota(jnp.int32, (tokens, tokens), 0)
+    s_index = lax.broadcasted_iota(jnp.int32, (tokens, tokens), 1)
+    lower = t_index >= s_index
+    for h in range(heads):
+        qh, kh, vh, dh = q[:, view(h)], k[:, view(h)], v[:, view(h)], do[:, view(h)]
+        diff = cum_col[:, h : h + 1] - cum_row[h : h + 1, :]
+        mask = jnp.where(lower, jnp.exp(jnp.where(lower, diff, 0.0)), 0.0)
+        scores = (contract(qh, kh, 1, 1) * mask).astype(BF)
+        dov = (contract(dh, vh, 1, 1) * mask).astype(BF)
+        intra[0, :, view(h)] = contract(scores, vh, 1, 0)
+        intra[1, :, view(h)] = contract(dov, kh, 1, 0)
+        intra[2, :, view(h)] = contract(dov, qh, 0, 0)
+        intra[3, :, view(h)] = contract(scores, dh, 0, 0)
+
     for copy in first:
         copy.wait()
-    state = jnp.zeros((rows, give.shape[2]), F32)
-    for k in range(n):
-        back[k, 0:rows] = state
-        state = got[k, 0:rows] + got[k, 2 * rows : 3 * rows] * state
-    state = jnp.zeros((rows, give.shape[2]), F32)
-    for k in range(n - 1, -1, -1):
-        back[k, rows : 2 * rows] = state
-        state = got[k, rows : 2 * rows] + got[k, 2 * rows : 3 * rows] * state
+    state = jnp.zeros((rows, size), F32)
+    for j in range(n):
+        back[j, 0:rows] = state
+        state = got[j, 0:rows] + got[j, 2 * rows : 3 * rows] * state
+    state = jnp.zeros((rows, size), F32)
+    for j in range(n - 1, -1, -1):
+        back[j, rows : 2 * rows] = state
+        state = got[j, rows : 2 * rows] + got[j, 2 * rows : 3 * rows] * state
     second = [push(back, land, s2, r2, r) for r in range(1, n)]
     for copy in second:
         copy.start()
     land[me] = back[me]
     for copy in second:
         copy.wait()
-    fwd_out[...] = land[:, 0:rows]
-    bwd_out[...] = land[:, rows : 2 * rows]
-
-
-def state_exchange(summary, backsum, block_decay, n):
-    heads, size, _ = summary.shape
+
+    headed = []
+    for h in range(heads):
+        lead, tail, _ = factors(h)
+        some = slice(h * per, (h + 1) * per)
+        state_in = land[some, 0:rows].reshape(size, size)
+        grad_in = land[some, rows : 2 * rows].reshape(size, size)
+        attended = intra[0, :, view(h)] + contract(q[:, view(h)], state_in, 1, 0) * lead
+        headed.append(rms_norm(attended, gain[:, view(h)]).astype(BF))
+        from_state = contract(do[:, view(h)], state_in, 1, 1)
+        grad_q[:, view(h)] = (intra[1, :, view(h)] + lead * from_state).astype(BF)
+        from_later = contract(v[:, view(h)], grad_in, 1, 1)
+        grad_k[:, view(h)] = (intra[2, :, view(h)] + tail * from_later).astype(BF)
+        from_later = contract(k[:, view(h)], grad_in, 1, 0)
+        grad_v[:, view(h)] = (intra[3, :, view(h)] + tail * from_later).astype(BF)
+    headed = jnp.concatenate(headed, axis=1)
+    cols = part.shape[2]
+    for z in range(part.shape[0]):
+        part[z] = contract(headed, w_out[:, z * cols : (z + 1) * cols], 1, 0).astype(BF)
+
+
+def attention_core(q, k, v, do, cum_decay, gain, w_out, n, n_head):
+    tokens, chans = q.shape
+    heads = cum_decay.shape[1]
+    size = chans // heads
     rows = heads * size // n
-    decay = jnp.broadcast_to(block_decay[:, None, None], (heads, n // heads * rows, size))
-    give = jnp.concatenate(
-        [
-            summary.reshape(n, rows, size),
-            backsum.reshape(n, rows, size),
-            decay.reshape(n, rows, size),
-        ],
-        axis=1,
-    )
-    out = jax.ShapeDtypeStruct((n, rows, size), F32)
     vmem = pl.BlockSpec(memory_space=pltpu.VMEM)
-    fwd, bwd = pl.pallas_call(
-        functools.partial(state_kernel, n, rows),
-        out_shape=(out, out),
-        in_specs=[vmem],
-        out_specs=(vmem, vmem),
+    grad = jax.ShapeDtypeStruct((tokens, chans), BF)
+    return pl.pallas_call(
+        functools.partial(core_kernel, n, heads),
+        out_shape=(
+            jax.ShapeDtypeStruct((n_head, tokens, w_out.shape[1] // n_head), BF),
+            grad,
+            grad,
+            grad,
+        ),
+        in_specs=[vmem] * 8,
+        out_specs=(vmem,) * 4,
         scratch_shapes=[
+            pltpu.VMEM((4, tokens, chans), F32),
+            pltpu.VMEM((n, 3 * rows, size), F32),
             pltpu.VMEM((n, 3 * rows, size), F32),
             pltpu.VMEM((n, 2 * rows, size), F32),
             pltpu.VMEM((n, 2 * rows, size), F32),
         ]
         + [pltpu.SemaphoreType.DMA((n - 1,))] * 4,
         compiler_params=pltpu.CompilerParams(collective_id=1, has_side_effects=True),
-        name="state_exchange",
-    )(give)
-    return fwd.reshape(heads, size, size), bwd.reshape(heads, size, size)
+        name="attention_core",
+    )(q, k, v, do, cum_decay, cum_decay.T, gain.reshape(1, chans), w_out)
 
 
 def hops(n, half, way):
@@ -537,7 +620,6 @@
     cap = 3 * tok_dev * TOP // (2 * experts)
     shards = n_head // EXP_CTX
     local_expert = my_head // shards
-    cols = width // n_head
     x_float = hidden_in.astype(F32)
     normed = rms_norm(x_float, gain_attn).astype(BF)
     mixed = jnp.einsum("ti,icj->tcj", normed, w_qkv, preferred_element_type=F32).astype(BF)
@@ -549,31 +631,21 @@
             conv_out + conv_w[offset] * padded[KERNEL - 1 - offset : KERNEL - 1 - offset + tok_dev]
         )
     activ = jax.nn.silu(conv_out)
-    shape3 = (tok_dev, heads_here, head_size)
-    queries = (activ[:, 0] * head_size ** (-0.5)).astype(BF).reshape(shape3)
-    keys = activ[:, 1].astype(BF).reshape(shape3)
-    vals = activ[:, 2].astype(BF).reshape(shape3)
-    cots = grad_core.reshape(shape3)
+    queries = (activ[:, 0] * head_size ** (-0.5)).astype(BF)
+    keys = activ[:, 1].astype(BF)
+    vals = activ[:, 2].astype(BF)
     steps = jnp.arange(tok_dev)
-    cum_decay = jnp.cumsum(log_decay, axis=0)
-    cum_t = cum_decay.T
-    diff = cum_t[:, :, None] - cum_t[:, None, :]
-    lower = (steps[:, None] >= steps[None, :])[None]
-    decay_mask = jnp.where(lower, jnp.exp(jnp.where(lower, diff, 0.0)), 0.0)
-    tail = jnp.exp(cum_decay[-1][None, :] - cum_decay)[:, :, None]
-    lead = jnp.exp(cum_decay)[:, :, None]
-    summary = mm("shd,she->hde", keys * tail, vals)
-    backsum = mm("thd,the->hde", queries * lead, cots)
-    block_decay = jnp.exp(cum_decay[-1])
-    state_in, grad_in = state_exchange(summary, backsum, block_decay, n_ctx)
-    scores = (mm("thd,shd->hts", queries, keys) * decay_mask).astype(BF)
-    attended = mm("hts,shd->thd", scores, vals) + mm("thd,hde->the", queries, state_in) * lead
-    headed = rms_norm(attended, norm_gain.reshape(heads_here, head_size)).reshape(tok_dev, chans)
-    partial_out = mm("ti,izc->ztc", headed, w_out.reshape(chans, n_head, cols)).astype(BF)
-    dov = (mm("thd,shd->hts", cots, vals) * decay_mask).astype(BF)
-    grad_q = mm("hts,shd->thd", dov, keys) + lead * mm("the,hde->thd", cots, state_in)
-    grad_k = mm("hts,thd->shd", dov, queries) + tail * mm("the,hde->thd", vals, grad_in)
-    grad_v = mm("hts,the->she", scores, cots) + tail * mm("thd,hde->the", keys, grad_in)
+    partial_out, grad_q, grad_k, grad_v = attention_core(
+        queries,
+        keys,
+        vals,
+        grad_core,
+        jnp.cumsum(log_decay, axis=0),
+        norm_gain,
+        w_out,
+        n_ctx,
+        n_head,
+    )
 
     wanted = EXP_CTX * jnp.arange(n_ctx, dtype=jnp.int32)[:, None] + local_expert
     chosen = expert_ids.T[:, None, :] == wanted[None]
@@ -596,9 +668,9 @@
     )
     return (
         layer_out,
-        grad_q.reshape(tok_dev, chans).astype(BF),
-        grad_k.reshape(tok_dev, chans).astype(BF),
-        grad_v.reshape(tok_dev, chans).astype(BF),
+        grad_q,
+        grad_k,
+        grad_v,
     )
 
 

time: 244 us -> 231 us (0.947)
  matrix products: 17.8 us -> 3.03 us
    dot_general x14 -> x1, matrix products: 15.4 us -> 0.76 us  [mm(): jnp.einsum(spec, a.astype(BF), b.astype(BF), preferred_element_type=F32)]
    unnamed x31 -> x21, local copies, waits for them, and re-layouts: 6.07 us -> 6.73 us
  transfers between devices with their start and end apart: 1 -> 1, of which waited for: 0 -> 0; matrix products, arithmetic and copies ran while one was open for 2% -> 4% of each run, Pallas kernels for 0% -> 0%
where the time goes in v4:
time: 231 us; the launch traced here: 229 us
  Pallas kernels  204 us (88%)
  local copies, waits for them, and re-layouts  11 us (5%)
  other arithmetic  7.89 us (3%)
  matrix products  3.03 us (1%)
    pallas_call x1, Pallas kernels, layer_tail(): pl.pallas_call(functools.partial(layer_kernel, n, n_head, cap, subs, grou...  181 us
    pallas_call x1, Pallas kernels, attention_core(): pl.pallas_call(functools.partial(core_kernel, n, heads), out_shape=(jax.S...  23.5 us
    unnamed x21, local copies, waits for them, and re-layouts  6.73 us
  transfers between devices with their start and end apart: 1, of which 0 were waited for; matrix products, arithmetic and copies ran while one was open for 4% of the time, Pallas kernels for 0%

profile of v4, /device:TPU:10, one launch (start us, length us, event | category | flops | bytes accessed | tf_op | source)
XLA Modules:
  0.0 229.0 jit_solution(15664616239538977516)
XLA Ops:
  0.6 1.7 fusion
  2.8 2.3 convolution_convert_fusion
  5.7 1.9 collective-permute-start
  7.7 1.5 fusion.16
  9.1 0.6 reduce-window.6
  9.7 0.7 slice_reduce_fusion
  10.5 0.8 reduce-window.9
  11.3 0.6 add_bitcast_fusion
  12.0 0.8 fusion.3.slot_ref
  12.8 0.7 copy_bitcast_fusion
  13.5 1.3 copy_bitcast_fusion.2
  14.8 1.4 fusion.11.weight_ref
  16.2 0.7 copy.33
  16.8 0.8 copy.20.cum_col
  17.6 0.8 maximum_convert_fusion
  18.4 1.2 fusion.15
  19.6 0.7 slice_bitcast_fusion
  20.3 0.7 fusion.13.q
  21.0 23.5 %attention_core.1 = (bf16[8,256,256]{2,1,0:T(8,128)(2,1)}, bf16[256,256]{1,0:T(8,128)(2,1)}, bf16[256,256]{1,0:T(8,128)(2,1)}, bf16[256,256]{1,0:T(8,128)(2,1)}) custom-call(bf16[256,256]{1,0:T(8,128)(2,1)} %fusion.13.q, bf16[256,256]{1,0:T(8,128)(2,1)} %get-tuple-element.15.k, bf16[256,256]{1,0:T(8,128)(2,1)} %get-tuple-element.14.v, bf16[256,256]{1,0:T(8,128)(2,1)} %do.1, ...), custom_call_target="tpu_custom_call" | custom-call | tf_op jit(solution)/shard_map/attention_core/pallas_call | solution.py:167
  44.5 180.9 %layer_tail.1 = bf16[256,256]{1,0:T(8,128)(2,1)} custom-call(bf16[8,256,256]{2,1,0:T(8,128)(2,1)} %get-tuple-element.8.part, bf16[256,2048]{1,0:T(8,128)(2,1)} %x_ref.1, f32[1,2048]{1,0:T(1,128)} %bitcast.44, s32[32,256]{1,0:T(8,128)} %fusion.3.slot_ref, f32[32,256]{1,0:T(8,128)} %fusion.11.weight_ref, bf16[2048,256]{1,0:T(8,128)(2,1)} %bitcast.37, ...), custom_call_target="tpu_custom_call" | custom-call | tf_op jit(solution)/shard_map/layer_tail/pallas_call | solution.py:559
  225.5 1.6 copy.38
  227.0 0.7 copy.39
  227.7 0.7 copy.40
  228.4 0.7 copy.41
  (20 shorter events, 1.3 us)
Async XLA Ops:
  0.6 2.2 copy-start
  2.8 6.3 %copy-start.6 = (f32[256,2]{0,1:T(2,128)S(1)}, f32[256,2]{0,1:T(2,128)}, u32[]{:S(2)}) copy-start(f32[256,2]{0,1:T(2,128)} %param.18) | copy-start | bytes 6148
  2.8 9.1 %copy-start.4 = (s32[256,8]{0,1:T(8,128)S(1)}, s32[256,8]{0,1:T(8,128)}, u32[]{:S(2)}) copy-start(s32[256,8]{0,1:T(8,128)} %param.22) | copy-start | bytes 24580
  5.7 11.9 %collective-permute-start = (bf16[3,3,256]{2,0,1:T(4,128)(2,1)}, bf16[3,3,256]{2,0,1:T(4,128)(2,1)}, u32[]{:S(2)}, u32[]{:S(2)}) collective-permute-start(bf16[3,3,256]{2,0,1:T(4,128)(2,1)} %slice.58), channel_id=1, source_target_pairs={{0,8},{8,16},{16,24},{24,32},{32,40},{40,48},{48,56},{56,64},{64,7... | collective-permute-start | bytes 13832 | tf_op jit(solution)/shard_map/ppermute | solution.py:21
  16.8 2.8 %copy-start.5 = (f32[1,2,2,128]{3,1,2,0:T(2,128)}, f32[1,2,2,128]{3,1,2,0:T(2,128)S(1)}, u32[]{:S(2)}) copy-start(f32[1,2,2,128]{3,1,2,0:T(2,128)S(1)} %copy.33) | copy-start | bytes 6148
  44.5 182.5 %copy-start.3 = (bf16[256,256]{1,0:T(8,128)(2,1)S(1)}, bf16[256,256]{1,0:T(8,128)(2,1)}, u32[]{:S(2)}) copy-start(bf16[256,256]{1,0:T(8,128)(2,1)} %get-tuple-element.31) | copy-start | bytes 393220
  44.5 183.2 %copy-start.2 = (bf16[256,256]{1,0:T(8,128)(2,1)S(1)}, bf16[256,256]{1,0:T(8,128)(2,1)}, u32[]{:S(2)}) copy-start(bf16[256,256]{1,0:T(8,128)(2,1)} %get-tuple-element.32) | copy-start | bytes 393220
  44.5 183.8 %copy-start.1 = (bf16[256,256]{1,0:T(8,128)(2,1)S(1)}, bf16[256,256]{1,0:T(8,128)(2,1)}, u32[]{:S(2)}) copy-start(bf16[256,256]{1,0:T(8,128)(2,1)} %get-tuple-element.33) | copy-start | bytes 393220

commit v5 on v4

--- a/solution.py
+++ b/solution.py
@@ -47,8 +47,8 @@
     k,
     v,
     do,
-    cum_col,
-    cum_row,
+    log_col,
+    log_row,
     gain,
     w_out,
     part,
@@ -83,6 +83,22 @@
             device_id_type=MESH,
         )
 
+    t_index = lax.broadcasted_iota(jnp.int32, (tokens, tokens), 0)
+    s_index = lax.broadcasted_iota(jnp.int32, (tokens, tokens), 1)
+    lower = t_index >= s_index
+    cum_col = jnp.dot(
+        jnp.where(lower, 1.0, 0.0),
+        log_col[...],
+        precision=lax.Precision.HIGHEST,
+        preferred_element_type=F32,
+    )
+    cum_row = jnp.dot(
+        log_row[...],
+        jnp.where(t_index <= s_index, 1.0, 0.0),
+        precision=lax.Precision.HIGHEST,
+        preferred_element_type=F32,
+    )
+
     def view(h):
         return slice(h * size, (h + 1) * size)
 
@@ -106,9 +122,6 @@
         copy.start()
     got[me] = give[me]
 
-    t_index = lax.broadcasted_iota(jnp.int32, (tokens, tokens), 0)
-    s_index = lax.broadcasted_iota(jnp.int32, (tokens, tokens), 1)
-    lower = t_index >= s_index
     for h in range(heads):
         qh, kh, vh, dh = q[:, view(h)], k[:, view(h)], v[:, view(h)], do[:, view(h)]
         diff = cum_col[:, h : h + 1] - cum_row[h : h + 1, :]
@@ -157,9 +170,9 @@
         part[z] = contract(headed, w_out[:, z * cols : (z + 1) * cols], 1, 0).astype(BF)
 
 
-def attention_core(q, k, v, do, cum_decay, gain, w_out, n, n_head):
+def attention_core(q, k, v, do, log_decay, gain, w_out, n, n_head):
     tokens, chans = q.shape
-    heads = cum_decay.shape[1]
+    heads = log_decay.shape[1]
     size = chans // heads
     rows = heads * size // n
     vmem = pl.BlockSpec(memory_space=pltpu.VMEM)
@@ -184,7 +197,7 @@
         + [pltpu.SemaphoreType.DMA((n - 1,))] * 4,
         compiler_params=pltpu.CompilerParams(collective_id=1, has_side_effects=True),
         name="attention_core",
-    )(q, k, v, do, cum_decay, cum_decay.T, gain.reshape(1, chans), w_out)
+    )(q, k, v, do, log_decay, log_decay.T, gain.reshape(1, chans), w_out)
 
 
 def hops(n, half, way):
@@ -640,7 +653,7 @@
         keys,
         vals,
         grad_core,
-        jnp.cumsum(log_decay, axis=0),
+        log_decay,
         norm_gain,
         w_out,
         n_ctx,

time: 231 us -> 227 us (0.983)
    unnamed x21 -> x17, local copies, waits for them, and re-layouts: 6.73 us -> 7.55 us
  transfers between devices with their start and end apart: 1 -> 1, of which waited for: 0 -> 0; matrix products, arithmetic and copies ran while one was open for 4% -> 3% of each run, Pallas kernels for 0% -> 0%
where the time goes in v5:
time: 227 us; the launch traced here: 225 us
  Pallas kernels  203 us (89%)
  local copies, waits for them, and re-layouts  10.3 us (5%)
  other arithmetic  5.82 us (3%)
  matrix products  3.03 us (1%)
    pallas_call x1, Pallas kernels, layer_tail(): pl.pallas_call(functools.partial(layer_kernel, n, n_head, cap, subs, grou...  179 us
    pallas_call x1, Pallas kernels, attention_core(): pl.pallas_call(functools.partial(core_kernel, n, heads), out_shape=(jax.S...  23.9 us
    unnamed x17, local copies, waits for them, and re-layouts  7.55 us
  transfers between devices with their start and end apart: 1, of which 0 were waited for; matrix products, arithmetic and copies ran while one was open for 3% of the time, Pallas kernels for 0%

profile of v5, /device:TPU:10, one launch (start us, length us, event | category | flops | bytes accessed | tf_op | source)
XLA Modules:
  0.0 224.6 jit_solution(17181877464657062180)
XLA Ops:
  0.6 0.0 copy-start
  0.6 1.7 fusion
  2.3 0.5 copy-done
  2.8 2.3 %convolution_convert_fusion = bf16[256,3,256]{2,0,1:T(8,128)(2,1)S(1)} fusion(bf16[2048,3,256]{2,0,1:T(8,128)(2,1)S(1)} %copy-done, bf16[256,2048]{1,0:T(8,128)(2,1)} %x_ref.1, f32[2048]{0:T(1024)} %param.15, f32[256]{0:T(256)S(1)} %add_rsqrt_fusion), kind=kOutput, calls=%fused_computation.5 | convolution fusion | flops 807600128 | bytes 4596736 | tf_op jit(solution)/shard_map/ti,icj->tcj/dot_general | solution.py:638
  5.1 0.6 slice.50
  5.7 1.9 collective-permute-start
  7.6 1.5 fusion.15
  9.1 0.1 compare_reduce_fusion
  9.2 0.8 fusion.3.slot_ref
  10.0 0.7 copy_bitcast_fusion
  10.7 1.3 copy_bitcast_fusion.2
  12.0 1.4 fusion.11.weight_ref
  13.4 1.5 copy.20.log_col
  14.8 0.0 collective-permute-done
  14.8 0.8 maximum_convert_fusion
  15.6 1.2 fusion.14
  16.8 0.7 slice_bitcast_fusion
  17.5 0.7 fusion.13.q
  18.2 23.9 %attention_core.1 = (bf16[8,256,256]{2,1,0:T(8,128)(2,1)}, bf16[256,256]{1,0:T(8,128)(2,1)}, bf16[256,256]{1,0:T(8,128)(2,1)}, bf16[256,256]{1,0:T(8,128)(2,1)}) custom-call(bf16[256,256]{1,0:T(8,128)(2,1)} %fusion.13.q, bf16[256,256]{1,0:T(8,128)(2,1)} %get-tuple-element.15.k, bf16[256,256]{1,0:T(8,128)(2,1)} %get-tuple-element.14.v, bf16[256,256]{1,0:T(8,128)(2,1)} %do.1, ...), custom_call_target="tpu_custom_call" | custom-call | tf_op jit(solution)/shard_map/attention_core/pallas_call | solution.py:180
  42.1 179.0 %layer_tail.1 = bf16[256,256]{1,0:T(8,128)(2,1)} custom-call(bf16[8,256,256]{2,1,0:T(8,128)(2,1)} %get-tuple-element.8.part, bf16[256,2048]{1,0:T(8,128)(2,1)} %x_ref.1, f32[1,2048]{1,0:T(1,128)} %bitcast.32, s32[32,256]{1,0:T(8,128)} %fusion.3.slot_ref, f32[32,256]{1,0:T(8,128)} %fusion.11.weight_ref, bf16[2048,256]{1,0:T(8,128)(2,1)} %bitcast.27, ...), custom_call_target="tpu_custom_call" | custom-call | tf_op jit(solution)/shard_map/layer_tail/pallas_call | solution.py:572
  221.1 1.6 copy.33
  222.7 0.7 copy.34
  223.3 0.7 copy.35
  224.0 0.7 copy.36
  (10 shorter events, 0.0 us)
Async XLA Ops:
  0.6 2.2 copy-start
  2.8 6.3 %copy-start.4 = (s32[256,8]{0,1:T(8,128)S(1)}, s32[256,8]{0,1:T(8,128)}, u32[]{:S(2)}) copy-start(s32[256,8]{0,1:T(8,128)} %param.22) | copy-start | bytes 24580
  5.7 9.1 %collective-permute-start = (bf16[3,3,256]{2,0,1:T(4,128)(2,1)}, bf16[3,3,256]{2,0,1:T(4,128)(2,1)}, u32[]{:S(2)}, u32[]{:S(2)}) collective-permute-start(bf16[3,3,256]{2,0,1:T(4,128)(2,1)} %slice.50), channel_id=1, source_target_pairs={{0,8},{8,16},{16,24},{24,32},{32,40},{40,48},{48,56},{56,64},{64,7... | collective-permute-start | bytes 13832 | tf_op jit(solution)/shard_map/ppermute | solution.py:21
  42.1 180.6 %copy-start.3 = (bf16[256,256]{1,0:T(8,128)(2,1)S(1)}, bf16[256,256]{1,0:T(8,128)(2,1)}, u32[]{:S(2)}) copy-start(bf16[256,256]{1,0:T(8,128)(2,1)} %get-tuple-element.29) | copy-start | bytes 393220
  42.1 181.2 %copy-start.2 = (bf16[256,256]{1,0:T(8,128)(2,1)S(1)}, bf16[256,256]{1,0:T(8,128)(2,1)}, u32[]{:S(2)}) copy-start(bf16[256,256]{1,0:T(8,128)(2,1)} %get-tuple-element.30) | copy-start | bytes 393220
  42.1 181.9 %copy-start.1 = (bf16[256,256]{1,0:T(8,128)(2,1)S(1)}, bf16[256,256]{1,0:T(8,128)(2,1)}, u32[]{:S(2)}) copy-start(bf16[256,256]{1,0:T(8,128)(2,1)} %get-tuple-element.31) | copy-start | bytes 393220
